TPU v7x, 32 devices: a whole 2x2x4 slice. The times are simulated.
32 devices in a mesh: gx: 4 (over x, core), gy: 8 (over z, y).
Axes of the slice: x: 2, y: 2, z: 4, core: 2. Of those that a mesh axis runs over, the one named last changes fastest.
Arguments:
- right_side: float32 [32, 64, 512], P('gx', 'gy'), may hold values from -18 to 18
- inverse_density: float32 [32, 64, 512], P('gx', 'gy'), may hold values from 0.01 to 10
Outputs:
- correction: float32 [32, 64, 512], P('gx', 'gy')
- residual: float32 [32, 64, 512], P('gx', 'gy')
All inputs are finite; a program needn't handle non-finite values.
Results may differ from a plain program's by a relative error of at most 0.00013.
Values sent between devices are 32-bit elements; how exact they have to be, the bound alone decides.
A program may use at most 64 MiB of HBM per device.

v0:
```python
import jax
import jax.numpy as jnp
from jax import lax
from jax.sharding import PartitionSpec as P

SWEEPS = 2
COARSE_SWEEPS = 8


def with_halo(cells, sides, width):
    for axis, dim in sides:
        count = lax.axis_size(axis)
        ends = count - 1
        head = lax.slice_in_dim(cells, 0, width, axis=dim)
        tail = lax.slice_in_dim(cells, cells.shape[dim] - width, cells.shape[dim], axis=dim)
        cells = jnp.concatenate(
            [
                lax.ppermute(tail, axis, [(i, (i + 1) % count) for i in range(ends)]),
                cells,
                lax.ppermute(head, axis, [((i + 1) % count, i) for i in range(ends)]),
            ],
            axis=dim,
        )
    return cells


def shift_down(values):
    return jnp.pad(values, ((0, 0), (0, 0), (1, 0)))[:, :, :-1]


def shift_up(values):
    return jnp.pad(values, ((0, 0), (0, 0), (0, 1)))[:, :, 1:]


def face_coefs(padded, scale):
    centre = padded[1:-1, 1:-1]
    faces = (
        scale * 0.5 * (centre + padded[:-2, 1:-1]),
        scale * 0.5 * (centre + padded[2:, 1:-1]),
        scale * 0.5 * (centre + padded[1:-1, :-2]),
        scale * 0.5 * (centre + padded[1:-1, 2:]),
        scale * 0.5 * (centre + shift_down(centre)),
        scale * 0.5 * (centre + shift_up(centre)),
    )
    diagonal = faces[0] + faces[1] + faces[2] + faces[3] + faces[4] + faces[5]
    return (faces, diagonal)


def neighbours(padded, faces):
    centre = padded[1:-1, 1:-1]
    total = faces[0] * padded[:-2, 1:-1] + faces[1] * padded[2:, 1:-1]
    total = total + faces[2] * padded[1:-1, :-2] + faces[3] * padded[1:-1, 2:]
    total = total + faces[4] * shift_down(centre) + faces[5] * shift_up(centre)
    return total


def red_cells(shape):
    along_x = lax.broadcasted_iota(jnp.int32, shape, 0)
    along_y = lax.broadcasted_iota(jnp.int32, shape, 1)
    along_z = lax.broadcasted_iota(jnp.int32, shape, 2)
    return (along_x + along_y + along_z) % 2 == 0


def restrict(values):
    size_x, size_y, size_z = values.shape
    blocks = values.reshape(size_x // 2, 2, size_y // 2, 2, size_z // 2, 2)
    return jnp.mean(blocks, axis=(1, 3, 5))


def prolong(values):
    return jnp.repeat(jnp.repeat(jnp.repeat(values, 2, axis=0), 2, axis=1), 2, axis=2)


def level_setup(density, scale):
    padded = with_halo(density, (("gx", 0), ("gy", 1)), 2)
    faces_ext, diag_ext = face_coefs(padded, scale)
    shape = diag_ext.shape
    along_x = lax.broadcasted_iota(jnp.int32, shape, 0)
    along_y = lax.broadcasted_iota(jnp.int32, shape, 1)
    rows_x = density.shape[0]
    rows_y = density.shape[1]
    global_x = lax.axis_index("gx") * rows_x - 1 + along_x
    global_y = lax.axis_index("gy") * rows_y - 1 + along_y
    inside = (
        (global_x >= 0)
        & (global_x < rows_x * lax.axis_size("gx"))
        & (global_y >= 0)
        & (global_y < rows_y * lax.axis_size("gy"))
    )
    corner = ((along_x == 0) | (along_x == shape[0] - 1)) & (
        (along_y == 0) | (along_y == shape[1] - 1)
    )
    usable = inside & jnp.logical_not(corner)
    diag_safe = diag_ext + (1.0 - usable.astype(jnp.float32))
    red_ext = red_cells(shape)
    red_usable = red_ext & usable
    faces_in = tuple((face[1:-1, 1:-1] for face in faces_ext))
    diag_in = diag_ext[1:-1, 1:-1]
    red_in = red_ext[1:-1, 1:-1]
    return (faces_ext, diag_safe, red_usable, faces_in, diag_in, red_in)


def smooth_level(field, source, level, sweeps):
    faces_ext, diag_safe, red_usable, faces_in, diag_in, red_in = level
    black_in = jnp.logical_not(red_in)
    for sweep in range(sweeps):
        for colour in (red_in, black_in):
            padded = with_halo(field, (("gx", 0), ("gy", 1)), 1)
            update = (source + neighbours(padded, faces_in)) / diag_in
            field = jnp.where(colour, update, field)
    return field


def level_residual(field, source, level):
    faces_in = level[3]
    diag_in = level[4]
    padded = with_halo(field, (("gx", 0), ("gy", 1)), 1)
    return source - (diag_in * field - neighbours(padded, faces_in))


def coarse_solve(density, source, sweeps):
    dens_all, source_all = (
        lax.all_gather(density, "gx", axis=0, tiled=True),
        lax.all_gather(source, "gx", axis=0, tiled=True),
    )
    padded = with_halo(dens_all, (("gy", 1),), 1)
    padded = jnp.pad(padded, ((1, 1), (0, 0), (0, 0)))
    faces, diagonal = face_coefs(padded, 0.0625)
    red = red_cells(diagonal.shape)
    field = jnp.zeros_like(source_all)
    for sweep in range(sweeps):
        for colour in (red, jnp.logical_not(red)):
            beside_all = with_halo(field, (("gy", 1),), 1)
            beside_all = jnp.pad(beside_all, ((1, 1), (0, 0), (0, 0)))
            update = (source_all + neighbours(beside_all, faces)) / diagonal
            field = jnp.where(colour, update, field)
    rows_x = density.shape[0]
    return lax.dynamic_slice_in_dim(field, lax.axis_index("gx") * rows_x, rows_x, 0)


def shards(right_side, inverse_density):
    dens_one = restrict(inverse_density)
    dens_two = restrict(dens_one)
    level_zero = level_setup(inverse_density, 1.0)
    level_one = level_setup(dens_one, 0.25)
    fine = smooth_level(jnp.zeros_like(right_side), right_side, level_zero, SWEEPS)
    source_one = restrict(level_residual(fine, right_side, level_zero))
    middle = smooth_level(jnp.zeros_like(source_one), source_one, level_one, SWEEPS)
    source_two = restrict(level_residual(middle, source_one, level_one))
    coarse = coarse_solve(dens_two, source_two, COARSE_SWEEPS)
    middle = smooth_level(middle + prolong(coarse), source_one, level_one, SWEEPS)
    fine = smooth_level(fine + prolong(middle), right_side, level_zero, SWEEPS)
    return (fine, level_residual(fine, right_side, level_zero))


def solution(mesh):
    in_specs = (P("gx", "gy", None), P("gx", "gy", None))
    out_specs = (P("gx", "gy", None), P("gx", "gy", None))
    return jax.shard_map(shards, mesh=mesh, in_specs=in_specs, out_specs=out_specs, check_vma=False)
```

profile of v0, /device:TPU:0, one launch (start us, length us, event | category | flops | bytes accessed | tf_op | source)
XLA Modules:
  0.0 511.1 jit_solution(3766428734550538434)
XLA Ops:
  4.3 5.1 %collective-permute-start.28 = (f32[1,4,256]{2,1,0:T(4,128)S(1)}, f32[1,4,256]{2,1,0:T(4,128)S(1)}, u32[]{:S(2)}, u32[]{:S(2)}) collective-permute-start(f32[1,4,256]{2,1,0:T(4,128)S(1)} %broadcast.253), channel_id=1, source_target_pairs={{0,8},{8,16},{16,24},{1,9},{9,17},{17,25},{2,10},{10,18},{18,26},{... | collective-permute-start | bytes 12296 | tf_op jit(solution)/shard_map/ppermute | solution.py:18
  11.5 4.3 collective-permute-start
  15.9 10.5 %reshape.36 = f32[4,2,4,2,256,2]{5,4,3,2,1,0:T(8,128)} reshape(f32[8,8,512]{2,1,0:T(8,128)} %param.3) | data formatting | bytes 262144 | tf_op jit(solution)/shard_map/reshape | solution.py:66
  34.9 4.5 collective-permute-start.24
  44.6 4.2 collective-permute-start.6
  50.7 4.2 collective-permute-done.7
  59.8 4.8 collective-permute-start.10
  82.3 4.5 collective-permute-start.26
  93.3 5.1 collective-permute-start.30
  99.9 5.2 %collective-permute-start.18 = (f32[10,1,512]{2,1,0:T(1,128)S(1)}, f32[10,1,512]{2,1,0:T(1,128)S(1)}, u32[]{:S(2)}, u32[]{:S(2)}) collective-permute-start(f32[10,1,512]{2,1,0:T(1,128)S(1)} %get-tuple-element.44), channel_id=1, source_target_pairs={{0,1},{1,2},{2,3},{3,4},{4,5},{5,6},{6,7},{8,9},{9,10},{10,11},{11... | collective-permute-start | bytes 61448 | tf_op jit(solution)/shard_map/ppermute | solution.py:18
  106.5 5.1 %collective-permute-done.19 = f32[10,1,512]{2,1,0:T(1,128)S(1)} collective-permute-done((f32[10,1,512]{2,1,0:T(1,128)S(1)}, f32[10,1,512]{2,1,0:T(1,128)S(1)}, u32[]{:S(2)}, u32[]{:S(2)}) %collective-permute-start.19) | collective-permute-done | bytes 20512 | tf_op jit(solution)/shard_map/ppermute | solution.py:20
  115.3 4.6 collective-permute-done.21
  119.9 4.8 collective-permute-start.22
  126.2 4.2 collective-permute-done.23
  130.7 9.7 %reshape.35 = f32[4,2,4,2,256,2]{5,4,3,2,1,0:T(8,128)} reshape(f32[8,8,512]{2,1,0:T(8,128)S(1)} %fusion.48) | data formatting | bytes 262144 | tf_op jit(solution)/shard_map/reshape | solution.py:66
  155.9 4.2 collective-permute-done.35
  164.6 4.5 collective-permute-start.50
  171.7 4.5 collective-permute-start.38
  177.6 6.9 %all_gather.7 = f32[8,2,128]{2,1,0:T(2,128)S(1)} all-gather(f32[2,2,128]{2,1,0:T(2,128)S(1)} %broadcast_multiply_fusion.2), channel_id=1, replica_groups=mesh['gx'=4,'gy'=8] {'gx'}, dimensions={0}, use_global_device_ids=true | all-gather | bytes 10240 | tf_op jit(solution)/shard_map/all_gather | solution.py:123
  188.1 4.5 collective-permute-start.48
  194.0 4.5 collective-permute-start.42
  199.9 4.9 collective-permute-done.43
  208.9 4.6 collective-permute-done.45
  213.6 4.8 collective-permute-start.46
  225.2 5.6 %all_gather.6 = f32[8,2,128]{2,1,0:T(2,128)S(1)} all-gather(f32[2,2,128]{2,1,0:T(2,128)S(1)} %broadcast_multiply_fusion.3), channel_id=1, replica_groups=mesh['gx'=4,'gy'=8] {'gx'}, dimensions={0}, use_global_device_ids=true | all-gather | bytes 10240 | tf_op jit(solution)/shard_map/all_gather | solution.py:124
  235.1 4.2 collective-permute-done.53
  239.4 4.5 collective-permute-start.54
  245.2 4.2 collective-permute-done.55
  253.6 4.2 collective-permute-done.57
  262.1 4.2 collective-permute-done.59
  270.6 4.2 collective-permute-done.61
  279.0 4.2 collective-permute-done.63
  287.5 4.2 collective-permute-done.65
  296.0 4.2 collective-permute-done.67
  304.4 4.2 collective-permute-done.69
  312.9 4.2 collective-permute-done.71
  321.3 4.2 collective-permute-done.73
  329.8 4.2 collective-permute-done.75
  338.3 4.2 collective-permute-done.77
  370.9 4.2 collective-permute-done.85
  386.2 4.2 collective-permute-done.89
  401.6 4.2 collective-permute-done.93
  416.9 4.2 collective-permute-done.97
  437.5 4.2 collective-permute-done.101
  454.4 4.2 collective-permute-done.105
  471.2 4.2 collective-permute-done.109
  488.1 4.2 collective-permute-done.113
  505.0 4.2 collective-permute-done.117
  (364 shorter events, 281.2 us)
Async XLA Ops:
  0.6 38.8 %collective-permute-start.4 = (f32[1,8,512]{2,1,0:T(8,128)S(1)}, f32[1,8,512]{2,1,0:T(8,128)S(1)}, u32[]{:S(2)}, u32[]{:S(2)}) collective-permute-start(f32[1,8,512]{2,1,0:T(8,128)S(1)} %broadcast.249), channel_id=1, source_target_pairs={{0,8},{8,16},{16,24},{1,9},{9,17},{17,25},{2,10},{10,18},{18,26},{... | collective-permute-start | bytes 49160 | tf_op jit(solution)/shard_map/ppermute | solution.py:18
  3.0 39.9 %collective-permute-start.5 = (f32[1,8,512]{2,1,0:T(8,128)S(1)}, f32[1,8,512]{2,1,0:T(8,128)S(1)}, u32[]{:S(2)}, u32[]{:S(2)}) collective-permute-start(f32[1,8,512]{2,1,0:T(8,128)S(1)} %broadcast.249), channel_id=1, source_target_pairs={{8,0},{16,8},{24,16},{9,1},{17,9},{25,17},{10,2},{18,10},{26,18},{... | collective-permute-start | bytes 49160 | tf_op jit(solution)/shard_map/ppermute | solution.py:20
  4.3 87.7 %collective-permute-start.28 = (f32[1,4,256]{2,1,0:T(4,128)S(1)}, f32[1,4,256]{2,1,0:T(4,128)S(1)}, u32[]{:S(2)}, u32[]{:S(2)}) collective-permute-start(f32[1,4,256]{2,1,0:T(4,128)S(1)} %broadcast.253), channel_id=1, source_target_pairs={{0,8},{8,16},{16,24},{1,9},{9,17},{17,25},{2,10},{10,18},{18,26},{... | collective-permute-start | bytes 12296 | tf_op jit(solution)/shard_map/ppermute | solution.py:18
  9.5 83.8 %collective-permute-start.29 = (f32[1,4,256]{2,1,0:T(4,128)S(1)}, f32[1,4,256]{2,1,0:T(4,128)S(1)}, u32[]{:S(2)}, u32[]{:S(2)}) collective-permute-start(f32[1,4,256]{2,1,0:T(4,128)S(1)} %broadcast.253), channel_id=1, source_target_pairs={{8,0},{16,8},{24,16},{9,1},{17,9},{25,17},{10,2},{18,10},{26,18},{... | collective-permute-start | bytes 12296 | tf_op jit(solution)/shard_map/ppermute | solution.py:20
  11.5 19.0 %collective-permute-start = (f32[2,8,512]{2,1,0:T(8,128)S(1)}, f32[2,8,512]{2,1,0:T(8,128)S(1)}, u32[]{:S(2)}, u32[]{:S(2)}) collective-permute-start(f32[2,8,512]{2,1,0:T(8,128)S(1)} %get-tuple-element.71), channel_id=1, source_target_pairs={{0,8},{8,16},{16,24},{1,9},{9,17},{17,25},{2,10},{10,18},{18,26},{... | collective-permute-start | bytes 98312 | tf_op jit(solution)/shard_map/ppermute | solution.py:18
  34.9 38.7 %collective-permute-start.24 = (f32[2,4,256]{2,1,0:T(4,128)S(1)}, f32[2,4,256]{2,1,0:T(4,128)S(1)}, u32[]{:S(2)}, u32[]{:S(2)}) collective-permute-start(f32[2,4,256]{2,1,0:T(4,128)S(1)} %get-tuple-element.115), channel_id=1, source_target_pairs={{0,8},{8,16},{16,24},{1,9},{9,17},{17,25},{2,10},{10,18},{18,26},{... | collective-permute-start | bytes 24584 | tf_op jit(solution)/shard_map/ppermute | solution.py:18
  42.9 6.0 %collective-permute-start.3 = (f32[12,2,512]{2,1,0:T(2,128)S(1)}, f32[12,2,512]{2,1,0:T(2,128)S(1)}, u32[]{:S(2)}, u32[]{:S(2)}) collective-permute-start(f32[12,2,512]{2,1,0:T(2,128)S(1)} %get-tuple-element.31), channel_id=1, source_target_pairs={{1,0},{2,1},{3,2},{4,3},{5,4},{6,5},{7,6},{9,8},{10,9},{11,10},{12... | collective-permute-start | bytes 147464 | tf_op jit(solution)/shard_map/ppermute | solution.py:20
  44.6 6.1 %collective-permute-start.6 = (f32[10,1,512]{2,1,0:T(1,128)S(1)}, f32[10,1,512]{2,1,0:T(1,128)S(1)}, u32[]{:S(2)}, u32[]{:S(2)}) collective-permute-start(f32[10,1,512]{2,1,0:T(1,128)S(1)} %get-tuple-element.50), channel_id=1, source_target_pairs={{0,1},{1,2},{2,3},{3,4},{4,5},{5,6},{6,7},{8,9},{9,10},{10,11},{11... | collective-permute-start | bytes 61448 | tf_op jit(solution)/shard_map/ppermute | solution.py:18
  48.9 6.1 %collective-permute-start.7 = (f32[10,1,512]{2,1,0:T(1,128)S(1)}, f32[10,1,512]{2,1,0:T(1,128)S(1)}, u32[]{:S(2)}, u32[]{:S(2)}) collective-permute-start(f32[10,1,512]{2,1,0:T(1,128)S(1)} %get-tuple-element.51), channel_id=1, source_target_pairs={{1,0},{2,1},{3,2},{4,3},{5,4},{6,5},{7,6},{9,8},{10,9},{11,10},{12... | collective-permute-start | bytes 61448 | tf_op jit(solution)/shard_map/ppermute | solution.py:20
  59.8 6.3 %collective-permute-start.10 = (f32[10,1,512]{2,1,0:T(1,128)S(1)}, f32[10,1,512]{2,1,0:T(1,128)S(1)}, u32[]{:S(2)}, u32[]{:S(2)}) collective-permute-start(f32[10,1,512]{2,1,0:T(1,128)S(1)} %get-tuple-element.48), channel_id=1, source_target_pairs={{0,1},{1,2},{2,3},{3,4},{4,5},{5,6},{6,7},{8,9},{9,10},{10,11},{11... | collective-permute-start | bytes 61448 | tf_op jit(solution)/shard_map/ppermute | solution.py:18
  64.7 5.7 %collective-permute-start.11 = (f32[10,1,512]{2,1,0:T(1,128)S(1)}, f32[10,1,512]{2,1,0:T(1,128)S(1)}, u32[]{:S(2)}, u32[]{:S(2)}) collective-permute-start(f32[10,1,512]{2,1,0:T(1,128)S(1)} %get-tuple-element.49), channel_id=1, source_target_pairs={{1,0},{2,1},{3,2},{4,3},{5,4},{6,5},{7,6},{9,8},{10,9},{11,10},{12... | collective-permute-start | bytes 61448 | tf_op jit(solution)/shard_map/ppermute | solution.py:20
  66.1 8.8 %collective-permute-start.25 = (f32[2,4,256]{2,1,0:T(4,128)S(1)}, f32[2,4,256]{2,1,0:T(4,128)S(1)}, u32[]{:S(2)}, u32[]{:S(2)}) collective-permute-start(f32[2,4,256]{2,1,0:T(4,128)S(1)} %get-tuple-element.116), channel_id=1, source_target_pairs={{8,0},{16,8},{24,16},{9,1},{17,9},{25,17},{10,2},{18,10},{26,18},{... | collective-permute-start | bytes 24584 | tf_op jit(solution)/shard_map/ppermute | solution.py:20
  77.6 9.2 %collective-permute-start.14 = (f32[10,1,512]{2,1,0:T(1,128)S(1)}, f32[10,1,512]{2,1,0:T(1,128)S(1)}, u32[]{:S(2)}, u32[]{:S(2)}) collective-permute-start(f32[10,1,512]{2,1,0:T(1,128)S(1)} %get-tuple-element.46), channel_id=1, source_target_pairs={{0,1},{1,2},{2,3},{3,4},{4,5},{5,6},{6,7},{8,9},{9,10},{10,11},{11... | collective-permute-start | bytes 61448 | tf_op jit(solution)/shard_map/ppermute | solution.py:18
  80.9 7.2 %collective-permute-start.15 = (f32[10,1,512]{2,1,0:T(1,128)S(1)}, f32[10,1,512]{2,1,0:T(1,128)S(1)}, u32[]{:S(2)}, u32[]{:S(2)}) collective-permute-start(f32[10,1,512]{2,1,0:T(1,128)S(1)} %get-tuple-element.47), channel_id=1, source_target_pairs={{1,0},{2,1},{3,2},{4,3},{5,4},{6,5},{7,6},{9,8},{10,9},{11,10},{12... | collective-permute-start | bytes 61448 | tf_op jit(solution)/shard_map/ppermute | solution.py:20
  82.3 16.2 %collective-permute-start.26 = (f32[8,2,256]{2,0,1:T(8,128)S(1)}, f32[8,2,256]{2,0,1:T(8,128)S(1)}, u32[]{:S(2)}, u32[]{:S(2)}) collective-permute-start(f32[8,2,256]{2,0,1:T(8,128)S(1)} %copy.727), channel_id=1, source_target_pairs={{0,1},{1,2},{2,3},{3,4},{4,5},{5,6},{6,7},{8,9},{9,10},{10,11},{11... | collective-permute-start | bytes 49160 | tf_op jit(solution)/shard_map/ppermute | solution.py:18
  86.9 12.9 %collective-permute-start.27 = (f32[8,2,256]{2,0,1:T(8,128)S(1)}, f32[8,2,256]{2,0,1:T(8,128)S(1)}, u32[]{:S(2)}, u32[]{:S(2)}) collective-permute-start(f32[8,2,256]{2,0,1:T(8,128)S(1)} %copy.728), channel_id=1, source_target_pairs={{1,0},{2,1},{3,2},{4,3},{5,4},{6,5},{7,6},{9,8},{10,9},{11,10},{12... | collective-permute-start | bytes 49160 | tf_op jit(solution)/shard_map/ppermute | solution.py:20
  88.4 11.4 %collective-permute-start.16 = (f32[1,8,512]{2,1,0:T(8,128)S(1)}, f32[1,8,512]{2,1,0:T(8,128)S(1)}, u32[]{:S(2)}, u32[]{:S(2)}) collective-permute-start(f32[1,8,512]{2,1,0:T(8,128)S(1)} %get-tuple-element.64), channel_id=1, source_target_pairs={{0,8},{8,16},{16,24},{1,9},{9,17},{17,25},{2,10},{10,18},{18,26},{... | collective-permute-start | bytes 49160 | tf_op jit(solution)/shard_map/ppermute | solution.py:18
  92.0 7.8 %collective-permute-start.17 = (f32[1,8,512]{2,1,0:T(8,128)S(1)}, f32[1,8,512]{2,1,0:T(8,128)S(1)}, u32[]{:S(2)}, u32[]{:S(2)}) collective-permute-start(f32[1,8,512]{2,1,0:T(8,128)S(1)} %get-tuple-element.65), channel_id=1, source_target_pairs={{8,0},{16,8},{24,16},{9,1},{17,9},{25,17},{10,2},{18,10},{26,18},{... | collective-permute-start | bytes 49160 | tf_op jit(solution)/shard_map/ppermute | solution.py:20
  93.3 51.2 %collective-permute-start.30 = (f32[6,1,256]{2,1,0:T(1,128)S(1)}, f32[6,1,256]{2,1,0:T(1,128)S(1)}, u32[]{:S(2)}, u32[]{:S(2)}) collective-permute-start(f32[6,1,256]{2,1,0:T(1,128)S(1)} %get-tuple-element.97), channel_id=1, source_target_pairs={{0,1},{1,2},{2,3},{3,4},{4,5},{5,6},{6,7},{8,9},{9,10},{10,11},{11... | collective-permute-start | bytes 18440 | tf_op jit(solution)/shard_map/ppermute | solution.py:18
  98.5 46.0 %collective-permute-start.31 = (f32[6,1,256]{2,1,0:T(1,128)S(1)}, f32[6,1,256]{2,1,0:T(1,128)S(1)}, u32[]{:S(2)}, u32[]{:S(2)}) collective-permute-start(f32[6,1,256]{2,1,0:T(1,128)S(1)} %get-tuple-element.98), channel_id=1, source_target_pairs={{1,0},{2,1},{3,2},{4,3},{5,4},{6,5},{7,6},{9,8},{10,9},{11,10},{12... | collective-permute-start | bytes 18440 | tf_op jit(solution)/shard_map/ppermute | solution.py:20
  99.9 6.6 %collective-permute-start.18 = (f32[10,1,512]{2,1,0:T(1,128)S(1)}, f32[10,1,512]{2,1,0:T(1,128)S(1)}, u32[]{:S(2)}, u32[]{:S(2)}) collective-permute-start(f32[10,1,512]{2,1,0:T(1,128)S(1)} %get-tuple-element.44), channel_id=1, source_target_pairs={{0,1},{1,2},{2,3},{3,4},{4,5},{5,6},{6,7},{8,9},{9,10},{10,11},{11... | collective-permute-start | bytes 61448 | tf_op jit(solution)/shard_map/ppermute | solution.py:18
  105.0 6.6 %collective-permute-start.19 = (f32[10,1,512]{2,1,0:T(1,128)S(1)}, f32[10,1,512]{2,1,0:T(1,128)S(1)}, u32[]{:S(2)}, u32[]{:S(2)}) collective-permute-start(f32[10,1,512]{2,1,0:T(1,128)S(1)} %get-tuple-element.45), channel_id=1, source_target_pairs={{1,0},{2,1},{3,2},{4,3},{5,4},{6,5},{7,6},{9,8},{10,9},{11,10},{12... | collective-permute-start | bytes 61448 | tf_op jit(solution)/shard_map/ppermute | solution.py:20
  113.9 6.0 %collective-permute-start.21 = (f32[1,8,512]{2,1,0:T(8,128)S(1)}, f32[1,8,512]{2,1,0:T(8,128)S(1)}, u32[]{:S(2)}, u32[]{:S(2)}) collective-permute-start(f32[1,8,512]{2,1,0:T(8,128)S(1)} %get-tuple-element.63), channel_id=1, source_target_pairs={{8,0},{16,8},{24,16},{9,1},{17,9},{25,17},{10,2},{18,10},{26,18},{... | collective-permute-start | bytes 49160 | tf_op jit(solution)/shard_map/ppermute | solution.py:20
  119.9 6.3 %collective-permute-start.22 = (f32[10,1,512]{2,1,0:T(1,128)S(1)}, f32[10,1,512]{2,1,0:T(1,128)S(1)}, u32[]{:S(2)}, u32[]{:S(2)}) collective-permute-start(f32[10,1,512]{2,1,0:T(1,128)S(1)} %get-tuple-element.42), channel_id=1, source_target_pairs={{0,1},{1,2},{2,3},{3,4},{4,5},{5,6},{6,7},{8,9},{9,10},{10,11},{11... | collective-permute-start | bytes 61448 | tf_op jit(solution)/shard_map/ppermute | solution.py:18
  124.8 5.7 %collective-permute-start.23 = (f32[10,1,512]{2,1,0:T(1,128)S(1)}, f32[10,1,512]{2,1,0:T(1,128)S(1)}, u32[]{:S(2)}, u32[]{:S(2)}) collective-permute-start(f32[10,1,512]{2,1,0:T(1,128)S(1)} %get-tuple-element.43), channel_id=1, source_target_pairs={{1,0},{2,1},{3,2},{4,3},{5,4},{6,5},{7,6},{9,8},{10,9},{11,10},{12... | collective-permute-start | bytes 61448 | tf_op jit(solution)/shard_map/ppermute | solution.py:20
  154.6 5.5 %collective-permute-start.35 = (f32[6,1,256]{2,1,0:T(1,128)S(1)}, f32[6,1,256]{2,1,0:T(1,128)S(1)}, u32[]{:S(2)}, u32[]{:S(2)}) collective-permute-start(f32[6,1,256]{2,1,0:T(1,128)S(1)} %get-tuple-element.96), channel_id=1, source_target_pairs={{1,0},{2,1},{3,2},{4,3},{5,4},{6,5},{7,6},{9,8},{10,9},{11,10},{12... | collective-permute-start | bytes 18440 | tf_op jit(solution)/shard_map/ppermute | solution.py:20
  160.2 11.5 %collective-permute-start.36 = (f32[1,4,256]{2,1,0:T(4,128)S(1)}, f32[1,4,256]{2,1,0:T(4,128)S(1)}, u32[]{:S(2)}, u32[]{:S(2)}) collective-permute-start(f32[1,4,256]{2,1,0:T(4,128)S(1)} %get-tuple-element.111), channel_id=1, source_target_pairs={{0,8},{8,16},{16,24},{1,9},{9,17},{17,25},{2,10},{10,18},{18,26},{... | collective-permute-start | bytes 12296 | tf_op jit(solution)/shard_map/ppermute | solution.py:18
  163.3 8.3 %collective-permute-start.37 = (f32[1,4,256]{2,1,0:T(4,128)S(1)}, f32[1,4,256]{2,1,0:T(4,128)S(1)}, u32[]{:S(2)}, u32[]{:S(2)}) collective-permute-start(f32[1,4,256]{2,1,0:T(4,128)S(1)} %get-tuple-element.112), channel_id=1, source_target_pairs={{8,0},{16,8},{24,16},{9,1},{17,9},{25,17},{10,2},{18,10},{26,18},{... | collective-permute-start | bytes 12296 | tf_op jit(solution)/shard_map/ppermute | solution.py:20
  164.6 55.1 %collective-permute-start.50 = (f32[8,1,128]{2,1,0:T(1,128)S(1)}, f32[8,1,128]{2,1,0:T(1,128)S(1)}, u32[]{:S(2)}, u32[]{:S(2)}) collective-permute-start(f32[8,1,128]{2,1,0:T(1,128)S(1)} %broadcast.257), channel_id=1, source_target_pairs={{0,1},{1,2},{2,3},{3,4},{4,5},{5,6},{6,7},{8,9},{9,10},{10,11},{11... | collective-permute-start | bytes 12296 | tf_op jit(solution)/shard_map/ppermute | solution.py:18
  169.2 50.5 %collective-permute-start.51 = (f32[8,1,128]{2,1,0:T(1,128)S(1)}, f32[8,1,128]{2,1,0:T(1,128)S(1)}, u32[]{:S(2)}, u32[]{:S(2)}) collective-permute-start(f32[8,1,128]{2,1,0:T(1,128)S(1)} %broadcast.257), channel_id=1, source_target_pairs={{1,0},{2,1},{3,2},{4,3},{5,4},{6,5},{7,6},{9,8},{10,9},{11,10},{12... | collective-permute-start | bytes 12296 | tf_op jit(solution)/shard_map/ppermute | solution.py:20
  171.7 12.8 %collective-permute-start.38 = (f32[6,1,256]{2,1,0:T(1,128)S(1)}, f32[6,1,256]{2,1,0:T(1,128)S(1)}, u32[]{:S(2)}, u32[]{:S(2)}) collective-permute-start(f32[6,1,256]{2,1,0:T(1,128)S(1)} %get-tuple-element.93), channel_id=1, source_target_pairs={{0,1},{1,2},{2,3},{3,4},{4,5},{5,6},{6,7},{8,9},{9,10},{10,11},{11... | collective-permute-start | bytes 18440 | tf_op jit(solution)/shard_map/ppermute | solution.py:18
  176.2 8.2 %collective-permute-start.39 = (f32[6,1,256]{2,1,0:T(1,128)S(1)}, f32[6,1,256]{2,1,0:T(1,128)S(1)}, u32[]{:S(2)}, u32[]{:S(2)}) collective-permute-start(f32[6,1,256]{2,1,0:T(1,128)S(1)} %get-tuple-element.94), channel_id=1, source_target_pairs={{1,0},{2,1},{3,2},{4,3},{5,4},{6,5},{7,6},{9,8},{10,9},{11,10},{12... | collective-permute-start | bytes 18440 | tf_op jit(solution)/shard_map/ppermute | solution.py:20
  184.6 8.1 %collective-permute-start.40 = (f32[1,4,256]{2,1,0:T(4,128)S(1)}, f32[1,4,256]{2,1,0:T(4,128)S(1)}, u32[]{:S(2)}, u32[]{:S(2)}) collective-permute-start(f32[1,4,256]{2,1,0:T(4,128)S(1)} %get-tuple-element.109), channel_id=1, source_target_pairs={{0,8},{8,16},{16,24},{1,9},{9,17},{17,25},{2,10},{10,18},{18,26},{... | collective-permute-start | bytes 12296 | tf_op jit(solution)/shard_map/ppermute | solution.py:18
  186.8 7.2 %collective-permute-start.41 = (f32[1,4,256]{2,1,0:T(4,128)S(1)}, f32[1,4,256]{2,1,0:T(4,128)S(1)}, u32[]{:S(2)}, u32[]{:S(2)}) collective-permute-start(f32[1,4,256]{2,1,0:T(4,128)S(1)} %get-tuple-element.110), channel_id=1, source_target_pairs={{8,0},{16,8},{24,16},{9,1},{17,9},{25,17},{10,2},{18,10},{26,18},{... | collective-permute-start | bytes 12296 | tf_op jit(solution)/shard_map/ppermute | solution.py:20
  188.1 10.5 %collective-permute-start.48 = (f32[8,1,128]{2,1,0:T(1,128)S(1)}, f32[8,1,128]{2,1,0:T(1,128)S(1)}, u32[]{:S(2)}, u32[]{:S(2)}) collective-permute-start(f32[8,1,128]{2,1,0:T(1,128)S(1)} %get-tuple-element.151), channel_id=1, source_target_pairs={{0,1},{1,2},{2,3},{3,4},{4,5},{5,6},{6,7},{8,9},{9,10},{10,11},{11... | collective-permute-start | bytes 12296 | tf_op jit(solution)/shard_map/ppermute | solution.py:18
  192.7 7.2 %collective-permute-start.49 = (f32[8,1,128]{2,1,0:T(1,128)S(1)}, f32[8,1,128]{2,1,0:T(1,128)S(1)}, u32[]{:S(2)}, u32[]{:S(2)}) collective-permute-start(f32[8,1,128]{2,1,0:T(1,128)S(1)} %get-tuple-element.152), channel_id=1, source_target_pairs={{1,0},{2,1},{3,2},{4,3},{5,4},{6,5},{7,6},{9,8},{10,9},{11,10},{12... | collective-permute-start | bytes 12296 | tf_op jit(solution)/shard_map/ppermute | solution.py:20
  194.0 5.9 %collective-permute-start.42 = (f32[6,1,256]{2,1,0:T(1,128)S(1)}, f32[6,1,256]{2,1,0:T(1,128)S(1)}, u32[]{:S(2)}, u32[]{:S(2)}) collective-permute-start(f32[6,1,256]{2,1,0:T(1,128)S(1)} %get-tuple-element.91), channel_id=1, source_target_pairs={{0,1},{1,2},{2,3},{3,4},{4,5},{5,6},{6,7},{8,9},{9,10},{10,11},{11... | collective-permute-start | bytes 18440 | tf_op jit(solution)/shard_map/ppermute | solution.py:18
  198.6 6.2 %collective-permute-start.43 = (f32[6,1,256]{2,1,0:T(1,128)S(1)}, f32[6,1,256]{2,1,0:T(1,128)S(1)}, u32[]{:S(2)}, u32[]{:S(2)}) collective-permute-start(f32[6,1,256]{2,1,0:T(1,128)S(1)} %get-tuple-element.92), channel_id=1, source_target_pairs={{1,0},{2,1},{3,2},{4,3},{5,4},{6,5},{7,6},{9,8},{10,9},{11,10},{12... | collective-permute-start | bytes 18440 | tf_op jit(solution)/shard_map/ppermute | solution.py:20
  207.5 6.0 %collective-permute-start.45 = (f32[1,4,256]{2,1,0:T(4,128)S(1)}, f32[1,4,256]{2,1,0:T(4,128)S(1)}, u32[]{:S(2)}, u32[]{:S(2)}) collective-permute-start(f32[1,4,256]{2,1,0:T(4,128)S(1)} %get-tuple-element.108), channel_id=1, source_target_pairs={{8,0},{16,8},{24,16},{9,1},{17,9},{25,17},{10,2},{18,10},{26,18},{... | collective-permute-start | bytes 12296 | tf_op jit(solution)/shard_map/ppermute | solution.py:20
  213.6 6.2 %collective-permute-start.46 = (f32[6,1,256]{2,1,0:T(1,128)S(1)}, f32[6,1,256]{2,1,0:T(1,128)S(1)}, u32[]{:S(2)}, u32[]{:S(2)}) collective-permute-start(f32[6,1,256]{2,1,0:T(1,128)S(1)} %get-tuple-element.89), channel_id=1, source_target_pairs={{0,1},{1,2},{2,3},{3,4},{4,5},{5,6},{6,7},{8,9},{9,10},{10,11},{11... | collective-permute-start | bytes 18440 | tf_op jit(solution)/shard_map/ppermute | solution.py:18
  218.4 5.5 %collective-permute-start.47 = (f32[6,1,256]{2,1,0:T(1,128)S(1)}, f32[6,1,256]{2,1,0:T(1,128)S(1)}, u32[]{:S(2)}, u32[]{:S(2)}) collective-permute-start(f32[6,1,256]{2,1,0:T(1,128)S(1)} %get-tuple-element.90), channel_id=1, source_target_pairs={{1,0},{2,1},{3,2},{4,3},{5,4},{6,5},{7,6},{9,8},{10,9},{11,10},{12... | collective-permute-start | bytes 18440 | tf_op jit(solution)/shard_map/ppermute | solution.py:20
  239.4 5.8 %collective-permute-start.54 = (f32[8,1,128]{2,1,0:T(1,128)S(1)}, f32[8,1,128]{2,1,0:T(1,128)S(1)}, u32[]{:S(2)}, u32[]{:S(2)}) collective-permute-start(f32[8,1,128]{2,1,0:T(1,128)S(1)} %get-tuple-element.147), channel_id=1, source_target_pairs={{0,1},{1,2},{2,3},{3,4},{4,5},{5,6},{6,7},{8,9},{9,10},{10,11},{11... | collective-permute-start | bytes 12296 | tf_op jit(solution)/shard_map/ppermute | solution.py:18
  369.5 5.5 %collective-permute-start.85 = (f32[6,1,256]{2,1,0:T(1,128)S(1)}, f32[6,1,256]{2,1,0:T(1,128)S(1)}, u32[]{:S(2)}, u32[]{:S(2)}) collective-permute-start(f32[6,1,256]{2,1,0:T(1,128)S(1)} %get-tuple-element.88), channel_id=1, source_target_pairs={{1,0},{2,1},{3,2},{4,3},{5,4},{6,5},{7,6},{9,8},{10,9},{11,10},{12... | collective-permute-start | bytes 18440 | tf_op jit(solution)/shard_map/ppermute | solution.py:20
  436.1 5.7 %collective-permute-start.101 = (f32[10,1,512]{2,1,0:T(1,128)S(1)}, f32[10,1,512]{2,1,0:T(1,128)S(1)}, u32[]{:S(2)}, u32[]{:S(2)}) collective-permute-start(f32[10,1,512]{2,1,0:T(1,128)S(1)} %get-tuple-element.41), channel_id=1, source_target_pairs={{1,0},{2,1},{3,2},{4,3},{5,4},{6,5},{7,6},{9,8},{10,9},{11,10},{12... | collective-permute-start | bytes 61448 | tf_op jit(solution)/shard_map/ppermute | solution.py:20
  452.9 5.7 %collective-permute-start.105 = (f32[10,1,512]{2,1,0:T(1,128)S(1)}, f32[10,1,512]{2,1,0:T(1,128)S(1)}, u32[]{:S(2)}, u32[]{:S(2)}) collective-permute-start(f32[10,1,512]{2,1,0:T(1,128)S(1)} %get-tuple-element.39), channel_id=1, source_target_pairs={{1,0},{2,1},{3,2},{4,3},{5,4},{6,5},{7,6},{9,8},{10,9},{11,10},{12... | collective-permute-start | bytes 61448 | tf_op jit(solution)/shard_map/ppermute | solution.py:20
  469.8 5.7 %collective-permute-start.109 = (f32[10,1,512]{2,1,0:T(1,128)S(1)}, f32[10,1,512]{2,1,0:T(1,128)S(1)}, u32[]{:S(2)}, u32[]{:S(2)}) collective-permute-start(f32[10,1,512]{2,1,0:T(1,128)S(1)} %get-tuple-element.37), channel_id=1, source_target_pairs={{1,0},{2,1},{3,2},{4,3},{5,4},{6,5},{7,6},{9,8},{10,9},{11,10},{12... | collective-permute-start | bytes 61448 | tf_op jit(solution)/shard_map/ppermute | solution.py:20
  486.6 5.7 %collective-permute-start.113 = (f32[10,1,512]{2,1,0:T(1,128)S(1)}, f32[10,1,512]{2,1,0:T(1,128)S(1)}, u32[]{:S(2)}, u32[]{:S(2)}) collective-permute-start(f32[10,1,512]{2,1,0:T(1,128)S(1)} %get-tuple-element.35), channel_id=1, source_target_pairs={{1,0},{2,1},{3,2},{4,3},{5,4},{6,5},{7,6},{9,8},{10,9},{11,10},{12... | collective-permute-start | bytes 61448 | tf_op jit(solution)/shard_map/ppermute | solution.py:20
  503.5 5.7 %collective-permute-start.117 = (f32[10,1,512]{2,1,0:T(1,128)S(1)}, f32[10,1,512]{2,1,0:T(1,128)S(1)}, u32[]{:S(2)}, u32[]{:S(2)}) collective-permute-start(f32[10,1,512]{2,1,0:T(1,128)S(1)} %get-tuple-element.33), channel_id=1, source_target_pairs={{1,0},{2,1},{3,2},{4,3},{5,4},{6,5},{7,6},{9,8},{10,9},{11,10},{12... | collective-permute-start | bytes 61448 | tf_op jit(solution)/shard_map/ppermute | solution.py:20
  (77 other events, 609.5 us)
where the time goes:
time: 515 us; the launch traced here: 511 us
  starting transfers between devices  268 us (52%)
  waiting for transfers between devices  178 us (35%)
  local copies, waits for them, and re-layouts  28 us (5%)
  other arithmetic  21.8 us (4%)
  blocking collectives  12.5 us (2%)
    ppermute x59, starting transfers between devices, with_halo(): lax.ppermute(tail, axis, [(i, (i + 1) % count) for i in range(ends)])  192 us
    ppermute x59, waiting for transfers between devices, with_halo(): lax.ppermute(head, axis, [((i + 1) % count, i) for i in range(ends)])  176 us
    ppermute x59, starting transfers between devices, with_halo(): lax.ppermute(head, axis, [((i + 1) % count, i) for i in range(ends)])  76.2 us
    reshape x3, local copies, waits for them, and re-layouts, restrict(): blocks = values.reshape(size_x // 2, 2, size_y // 2, 2, size_z // 2, 2)  21.2 us
  transfers between devices with their start and end apart: 118, of which 55 were waited for; matrix products, arithmetic and copies ran while one was open for 6% of the time, Pallas kernels for 0%

commit v1 on v0

v1 whole, which is shorter than its diff:
```python
import functools

import jax
import jax.numpy as jnp
from jax import lax
from jax.experimental import pallas as pl
from jax.experimental.pallas import tpu as pltpu
from jax.sharding import PartitionSpec as P

SWEEPS = 2
COARSE_SWEEPS = 8
MESH = pl.DeviceIdType.MESH
LANES = 128
F32 = jnp.float32


def iota(shape, dim):
    return lax.broadcasted_iota(jnp.int32, shape, dim)


def lane_prev(a):
    return jnp.where(iota(a.shape, 2) == 0, 0.0, pltpu.roll(a, 1, 2))


def lane_next(a):
    return jnp.where(iota(a.shape, 2) == LANES - 1, 0.0, pltpu.roll(a, LANES - 1, 2))


def row_prev(a, halo):
    return jnp.where(iota(a.shape, 1) == 0, halo, pltpu.roll(a, 1, 1)) if a.shape[1] % 8 == 0 else jnp.concatenate(
        [halo, a[:, :-1]], axis=1
    )


def row_next(a, halo):
    rows = a.shape[1]
    return jnp.where(iota(a.shape, 1) == rows - 1, halo, pltpu.roll(a, rows - 1, 1)) if rows % 8 == 0 else jnp.concatenate(
        [a[:, 1:], halo], axis=1
    )


def even_cells(shape):
    return (iota(shape, 0) + iota(shape, 1)) % 2 == 0


def z_other(o, colour):
    even = even_cells(o[0].shape)
    low = even if colour == 0 else jnp.logical_not(even)
    last = len(o) - 1
    out = []
    for b in range(last + 1):
        before = o[b - 1] if b > 0 else lane_prev(o[last])
        after = o[b + 1] if b < last else lane_next(o[0])
        out.append(jnp.where(low, before, after))
    return out


def around(o, halo, colour):
    xlo, xhi, ylo, yhi = halo
    zo = z_other(o, colour)
    out = []
    for b, a in enumerate(o):
        out.append(
            (
                jnp.concatenate([xlo[b], a[:-1]], axis=0),
                jnp.concatenate([a[1:], xhi[b]], axis=0),
                row_prev(a, ylo[b]),
                row_next(a, yhi[b]),
                a,
                zo[b],
            )
        )
    return out


def split_even(zero, one):
    even = even_cells(zero.shape)
    return jnp.where(even, zero, one), jnp.where(even, one, zero)


def pair_rows(a):
    rows = a.shape[1] // 2
    a = a.reshape(a.shape[0] // 2, 2, a.shape[1], LANES)
    a = a[:, 0] + a[:, 1]
    pick = iota((a.shape[0], rows, LANES), 1)
    out = a[:, 0:1] + a[:, 1:2]
    out = jnp.broadcast_to(out, pick.shape)
    for j in range(1, rows):
        out = jnp.where(pick == j, a[:, 2 * j : 2 * j + 1] + a[:, 2 * j + 1 : 2 * j + 2], out)
    return out * 0.125


def double_rows(a):
    x, rows, _ = a.shape
    pick = iota((x, 2 * rows, LANES), 1) // 2
    out = jnp.broadcast_to(a[:, 0:1], pick.shape)
    for j in range(1, rows):
        out = jnp.where(pick == j, a[:, j : j + 1], out)
    return jnp.concatenate([out[i // 2 : i // 2 + 1] for i in range(2 * x)], axis=0)


def three(x):
    high = x.astype(jnp.bfloat16)
    rest = x - high.astype(F32)
    middle = rest.astype(jnp.bfloat16)
    low = (rest - middle.astype(F32)).astype(jnp.bfloat16)
    return high, middle, low


def permute(x, matrix, side):
    parts = [
        lax.dot_general(part, matrix, (((1,), (side,)), ((), ())), preferred_element_type=F32)
        for part in three(x)
    ]
    return (parts[0] + parts[1]) + parts[2]


def kernel(nx, ny, g_ref, c_ref, v_out, r_out, perm, k0, k1, k2, sx0, sy0, rx0, ry0, sx1, sy1, rx1, ry1,
           ga, gb, vc, cw, sem0, sem1, semx, semy):
    gx, gy = lax.axis_index("gx"), lax.axis_index("gy")
    has = (gx > 0, gx < nx - 1, gy > 0, gy < ny - 1)
    peer = ({"gx": gx - 1}, {"gx": gx + 1}, {"gy": gy - 1}, {"gy": gy + 1})
    bufs = ((sx0, sy0, rx0, ry0, sem0), (sx1, sy1, rx1, ry1, sem1))

    for rx, ry in ((rx0, ry0), (rx1, ry1)):
        for d in range(4):
            ref = (rx, ry)[d // 2]

            @pl.when(jnp.logical_not(has[d]))
            def _():
                ref[:, d % 2] = jnp.zeros((ref.shape[0],) + ref.shape[2:], F32)

    barrier = pltpu.get_barrier_semaphore()
    for s in range(1, nx):
        pl.semaphore_signal(barrier, inc=1, device_id={"gx": lax.rem(gx + s, nx)}, device_id_type=MESH)
    for s in range(1, ny):
        pl.semaphore_signal(barrier, inc=1, device_id={"gy": lax.rem(gy + s, ny)}, device_id_type=MESH)

    size_z = 4 * LANES
    row, col = iota((size_z, size_z), 0), iota((size_z, size_z), 1)
    perm[...] = (row == 4 * (col % LANES) + col // LANES).astype(F32).astype(jnp.bfloat16)

    def unpack(ref):
        flat = permute(ref[...].reshape(-1, size_z), perm[...], 0)
        quarters = [flat[:, q * LANES : (q + 1) * LANES].reshape(ref.shape[0], ref.shape[1], LANES) for q in range(4)]
        pairs = [split_even(quarters[2 * b], quarters[2 * b + 1]) for b in range(2)]
        return [pairs[b][0] for b in range(2)], [pairs[b][1] for b in range(2)]

    def pack(ref, red, black):
        quarters = []
        for b in range(2):
            quarters.extend(split_even(red[b], black[b]))
        flat = jnp.concatenate([q.reshape(-1, LANES) for q in quarters], axis=1)
        ref[...] = permute(flat, perm[...], 1).reshape(ref.shape)

    def coarsen(red, black):
        pair = [pair_rows(red[b] + black[b]) for b in range(len(red))]
        if len(pair) == 1:
            return pair[0]
        first, second = split_even(pair[0], pair[1])
        return [first], [second]

    def copy(level, ph, d, into=False):
        sx, sy, rx, ry, sem = bufs[level]
        send, recv = (sx, rx) if d < 2 else (sy, ry)
        lands = d if into else d + 1 - 2 * (d % 2)
        return pltpu.make_async_remote_copy(
            src_ref=send.at[ph, d % 2], dst_ref=recv.at[ph, lands % 2], send_sem=sem.at[0, ph, d],
            recv_sem=sem.at[1, ph, lands], device_id=peer[d], device_id_type=MESH)

    def start(level, ph, o):
        sx, sy = bufs[level][:2]
        for b, a in enumerate(o):
            sx[ph, 0, b] = a[:1]
            sx[ph, 1, b] = a[-1:]
            sy[ph, 0, b] = a[:, :1]
            sy[ph, 1, b] = a[:, -1:]
        for d in range(4):
            @pl.when(has[d])
            def _():
                copy(level, ph, d).start()

    def finish(level, ph):
        for d in range(4):
            @pl.when(has[d])
            def _():
                copy(level, ph, d, into=True).wait_recv()
                copy(level, ph, d).wait_send()
        rx, ry = bufs[level][2:4]
        groups = range(rx.shape[2])
        return [[ref[ph, side, b] for b in groups] for ref in (rx, ry) for side in range(2)]

    phase = [0, 0]

    def swap(level, o):
        ph = phase[level]
        phase[level] += 1
        start(level, ph, o)
        return finish(level, ph)

    def gather_copy(stage, s):
        if stage == 0:
            return pltpu.make_async_remote_copy(
                src_ref=ga.at[gx], dst_ref=ga.at[gx], send_sem=semx.at[0, s], recv_sem=semx.at[1, s],
                device_id={"gx": lax.rem(gx + s, nx)}, device_id_type=MESH)
        return pltpu.make_async_remote_copy(
            src_ref=gb.at[gy], dst_ref=gb.at[gy], send_sem=semy.at[0, s], recv_sem=semy.at[1, s],
            device_id={"gy": lax.rem(gy + s, ny)}, device_id_type=MESH)

    def gather(dens, source):
        ga[gx, 0] = dens
        ga[gx, 1] = source
        for s in range(1, nx):
            gather_copy(0, s).start()
        for s in range(1, nx):
            src = lax.rem(gx + nx - s, nx)
            pltpu.make_async_remote_copy(
                src_ref=ga.at[src], dst_ref=ga.at[src], send_sem=semx.at[0, s], recv_sem=semx.at[1, s],
                device_id={"gx": src}, device_id_type=MESH).wait_recv()
            gather_copy(0, s).wait_send()
        for i in range(nx):
            gb[gy, 0, 2 * i : 2 * i + 2] = ga[i, 0]
            gb[gy, 1, 2 * i : 2 * i + 2] = ga[i, 1]
        for s in range(1, ny):
            gather_copy(1, s).start()
        for s in range(1, ny):
            src = lax.rem(gy + ny - s, ny)
            pltpu.make_async_remote_copy(
                src_ref=gb.at[src], dst_ref=gb.at[src], send_sem=semy.at[0, s], recv_sem=semy.at[1, s],
                device_id={"gy": src}, device_id_type=MESH).wait_recv()
            gather_copy(1, s).wait_send()

    def setup(kref, own, other, halo, colour, scale):
        for b, near in enumerate(around(other, halo, colour)):
            total = None
            for f in range(6):
                face = (scale * 0.5) * (own[b] + near[f])
                kref[colour, b, f] = face
                total = face if total is None else total + face
            kref[colour, b, 6] = total
            kref[colour, b, 7] = 1.0 / total

    def weigh(kref, o, halo, colour):
        out = []
        for b, near in enumerate(around(o, halo, colour)):
            total = kref[colour, b, 0] * near[0]
            for f in range(1, 6):
                total = total + kref[colour, b, f] * near[f]
            out.append(total)
        return out

    def update(kref, g, o, halo, colour):
        n = weigh(kref, o, halo, colour)
        return [(g[b] + n[b]) * kref[colour, b, 7] for b in range(len(n))]

    def remainder(kref, g, v, o, halo, colour):
        n = weigh(kref, o, halo, colour)
        return [g[b] - (kref[colour, b, 6] * v[b] - n[b]) for b in range(len(n))]

    def smooth(level, kref, g, v, sweeps):
        zero = v is None
        red, black = (None, None) if zero else v
        for sweep in range(sweeps):
            if zero and sweep == 0:
                red = [g[0][b] * kref[0, b, 7] for b in range(len(g[0]))]
            else:
                red = update(kref, g[0], black, swap(level, black), 0)
            red_halo = swap(level, red)
            black = update(kref, g[1], red, red_halo, 1)
        return red, black, red_halo

    def residual(level, kref, g, v):
        red, black, red_halo = v
        left = remainder(kref, g[1], black, red, red_halo, 1)
        return remainder(kref, g[0], red, black, swap(level, black), 0), left

    pl.semaphore_wait(barrier, nx - 1 + ny - 1)

    dens = unpack(c_ref)
    for c in range(2):
        start(0, c, dens[c])
    dens_one = coarsen(*dens)
    for c in range(2):
        start(1, c, dens_one[c])
    dens_two = coarsen(*dens_one)
    source = unpack(g_ref)
    for level, kref, d, scale in ((0, k0, dens, 1.0), (1, k1, dens_one, 0.25)):
        halos = [finish(level, c) for c in range(2)]
        phase[level] = 2
        for c in range(2):
            setup(kref, d[c], d[1 - c], halos[1 - c], c, scale)

    fine = smooth(0, k0, source, None, SWEEPS)
    source_one = coarsen(*residual(0, k0, source, fine))
    middle = smooth(1, k1, source_one, None, SWEEPS)
    source_two = coarsen(*residual(1, k1, source_one, middle))

    gather(dens_two, source_two)
    for j in range(ny):
        cw[0, :, 2 * j : 2 * j + 2] = gb[j, 0]
        cw[1, :, 2 * j : 2 * j + 2] = gb[j, 1]

    def sides(a):
        plane = jnp.zeros_like(a[:1])
        line = jnp.zeros_like(a[:, :1])
        return (
            jnp.concatenate([plane, a[:-1]], axis=0), jnp.concatenate([a[1:], plane], axis=0),
            row_prev(a, line), row_next(a, line), lane_prev(a), lane_next(a))

    centre = cw[0]
    total = None
    for f, near in enumerate(sides(centre)):
        face = 0.03125 * (centre + near)
        k2[f] = face
        total = face if total is None else total + face
    k2[6] = 1.0 / total
    shape = centre.shape
    red_two = (iota(shape, 0) + iota(shape, 1) + iota(shape, 2)) % 2 == 0
    cw[0] = jnp.zeros(shape, F32)

    def half(red):
        field = cw[0]
        total = cw[1]
        for f, near in enumerate(sides(field)):
            total = total + k2[f] * near
        total = total * k2[6]
        cw[0] = jnp.where(red_two, total, field) if red else jnp.where(red_two, field, total)

    def sweep(i, carry):
        half(True)
        half(False)
        return carry

    lax.fori_loop(0, COARSE_SWEEPS, sweep, 0)
    field = cw[0]
    for j in range(ny):
        vc[j] = field[:, 2 * j : 2 * j + 2]
    add = double_rows(vc[gy, pl.ds(2 * gx, 2)])
    middle = smooth(1, k1, source_one, [[v[0] + add] for v in middle[:2]], SWEEPS)
    adds = [double_rows(a) for a in split_even(middle[0][0], middle[1][0])]
    fine = smooth(0, k0, source, [[v[b] + adds[b] for b in range(2)] for v in fine[:2]], SWEEPS)
    pack(v_out, fine[0], fine[1])
    left = residual(0, k0, source, fine)
    pack(r_out, left[0], left[1])


def solution(mesh):
    nx, ny = mesh.shape["gx"], mesh.shape["gy"]

    def shards(right_side, inverse_density):
        x, y, z = right_side.shape
        x1, y1 = x // 2, y // 2
        p0, p1 = 4 * SWEEPS + 3, 4 * SWEEPS + 2
        halo0 = [pltpu.VMEM((p0, 2, 2, 1, y, LANES), F32), pltpu.VMEM((p0, 2, 2, x, 1, LANES), F32)]
        halo1 = [pltpu.VMEM((p1, 2, 1, 1, y1, LANES), F32), pltpu.VMEM((p1, 2, 1, x1, 1, LANES), F32)]
        out = jax.ShapeDtypeStruct(right_side.shape, F32)
        return pl.pallas_call(
            functools.partial(kernel, nx, ny),
            out_shape=(out, out),
            in_specs=[pl.BlockSpec(memory_space=pltpu.VMEM)] * 2,
            out_specs=(pl.BlockSpec(memory_space=pltpu.VMEM),) * 2,
            scratch_shapes=[
                pltpu.VMEM((z, z), jnp.bfloat16),
                pltpu.VMEM((2, 2, 8, x, y, LANES), F32),
                pltpu.VMEM((2, 1, 8, x1, y1, LANES), F32),
                pltpu.VMEM((7, nx * x // 4, ny * y // 4, LANES), F32),
                *halo0, *halo0, *halo1, *halo1,
                pltpu.VMEM((nx, 2, x // 4, y // 4, LANES), F32),
                pltpu.VMEM((ny, 2, nx * x // 4, y // 4, LANES), F32),
                pltpu.VMEM((ny, nx * x // 4, y // 4, LANES), F32),
                pltpu.VMEM((2, nx * x // 4, ny * y // 4, LANES), F32),
                pltpu.SemaphoreType.DMA((2, p0, 4)),
                pltpu.SemaphoreType.DMA((2, p1, 4)),
                pltpu.SemaphoreType.DMA((2, nx)),
                pltpu.SemaphoreType.DMA((2, ny)),
            ],
            compiler_params=pltpu.CompilerParams(
                collective_id=0, has_side_effects=True, vmem_limit_bytes=48 * 1024 * 1024
            ),
        )(right_side, inverse_density)

    spec = P("gx", "gy", None)
    return jax.shard_map(shards, mesh=mesh, in_specs=(spec, spec), out_specs=(spec, spec), check_vma=False)
```

time: 515 us -> 79 us (0.15)
  starting transfers between devices: 268 us -> 0 us
  waiting for transfers between devices: 178 us -> 0 us
  Pallas kernels: 0 us -> 75.1 us
  local copies, waits for them, and re-layouts: 28 us -> 3.11 us
  other arithmetic: 21.8 us -> 0 us
  blocking collectives: 12.5 us -> 0 us
    ppermute x118 -> x0, starting transfers between devices: 268 us -> none  [the longest x59 192 us: with_halo(): lax.ppermute(tail, axis, [(i, (i + 1) % count) for i in range(ends)])]
    ppermute x118 -> x0, waiting for transfers between devices: 178 us -> none  [the longest x59 176 us: with_halo(): lax.ppermute(head, axis, [((i + 1) % count, i) for i in range(ends)])]
    pallas_call x0 -> x1, Pallas kernels: none -> 75.1 us  [shards(): pl.pallas_call(functools.partial(kernel, nx, ny), out_shape=(out, out), i...]
    reshape x8 -> x0, local copies, waits for them, and re-layouts: 24.3 us -> none  [the longest x3 21.2 us: restrict(): blocks = values.reshape(size_x // 2, 2, size_y // 2, 2, size_z // 2, 2)]
    all_gather x2 -> x0, blocking collectives: 12.5 us -> none  [the longest x1 6.9 us: coarse_solve(): lax.all_gather(density, 'gx', axis=0, tiled=True)]
    reduce_sum x4 -> x0, other arithmetic: 8.44 us -> none  [restrict(): return jnp.mean(blocks, axis=(1, 3, 5))]
    select_n x32 -> x0, other arithmetic: 8.43 us -> none  [the longest x16 7.01 us: smooth_level(): field = jnp.where(colour, update, field)]
  transfers between devices with their start and end apart: 118 -> 0, of which waited for: 55 -> 0; matrix products, arithmetic and copies ran while one was open for 6% -> 0% of each run, Pallas kernels for 0% -> 0%
where the time goes in v1:
time: 79 us; the launch traced here: 78.8 us
  Pallas kernels  75.1 us (95%)
  local copies, waits for them, and re-layouts  3.11 us (4%)
    pallas_call x1, Pallas kernels, shards(): pl.pallas_call(functools.partial(kernel, nx, ny), out_shape=(out, out), i...  75.1 us
    unnamed x6, local copies, waits for them, and re-layouts  3.11 us

profile of v1, /device:TPU:0, one launch (start us, length us, event | category | flops | bytes accessed | tf_op | source)
XLA Modules:
  0.0 78.8 jit_solution(9145443177232627670)
XLA Ops:
  0.6 0.0 copy-start
  0.6 0.9 %copy-done = f32[8,8,512]{2,1,0:T(8,128)S(1)} copy-done((f32[8,8,512]{2,1,0:T(8,128)S(1)}, f32[8,8,512]{2,1,0:T(8,128)}, u32[]{:S(2)}) %copy-start) | copy-done | bytes 131096
  1.5 0.0 copy-start.1
  1.5 0.9 %copy-done.1 = f32[8,8,512]{2,1,0:T(8,128)S(1)} copy-done((f32[8,8,512]{2,1,0:T(8,128)S(1)}, f32[8,8,512]{2,1,0:T(8,128)}, u32[]{:S(2)}) %copy-start.1) | copy-done | bytes 131096
  2.4 75.1 %shard_map.41 = (f32[8,8,512]{2,1,0:T(8,128)S(1)}, f32[8,8,512]{2,1,0:T(8,128)S(1)}) custom-call(f32[8,8,512]{2,1,0:T(8,128)S(1)} %copy-done, f32[8,8,512]{2,1,0:T(8,128)S(1)} %copy-done.1), custom_call_target="tpu_custom_call" | custom-call | tf_op jit(solution)/shard_map/pallas_call | solution.py:357
  77.5 0.7 copy.6
  78.2 0.7 copy.7
Async XLA Ops:
  0.6 0.9 %copy-start = (f32[8,8,512]{2,1,0:T(8,128)S(1)}, f32[8,8,512]{2,1,0:T(8,128)}, u32[]{:S(2)}) copy-start(f32[8,8,512]{2,1,0:T(8,128)} %g_ref.1) | copy-start | bytes 393220
  1.5 0.9 %copy-start.1 = (f32[8,8,512]{2,1,0:T(8,128)S(1)}, f32[8,8,512]{2,1,0:T(8,128)}, u32[]{:S(2)}) copy-start(f32[8,8,512]{2,1,0:T(8,128)} %c_ref.1) | copy-start | bytes 393220

commit v2 on v1

--- a/solution.py
+++ b/solution.py
@@ -43,8 +43,12 @@
     return (iota(shape, 0) + iota(shape, 1)) % 2 == 0
 
 
-def z_other(o, colour):
-    even = even_cells(o[0].shape)
+REGION_Y = 16
+
+
+def z_other(o, colour, first):
+    shape = o[0].shape
+    even = (iota(shape, 0) + iota(shape, 1)) % 2 == first % 2
     low = even if colour == 0 else jnp.logical_not(even)
     last = len(o) - 1
     out = []
@@ -55,22 +59,22 @@
     return out
 
 
-def around(o, halo, colour):
-    xlo, xhi, ylo, yhi = halo
-    zo = z_other(o, colour)
-    out = []
-    for b, a in enumerate(o):
-        out.append(
-            (
-                jnp.concatenate([xlo[b], a[:-1]], axis=0),
-                jnp.concatenate([a[1:], xhi[b]], axis=0),
-                row_prev(a, ylo[b]),
-                row_next(a, yhi[b]),
-                a,
-                zo[b],
-            )
+def around(ref, colour, x0, x1):
+    other = 1 - colour
+    groups = range(ref.shape[1])
+    mid = [ref[other, b, x0:x1] for b in groups]
+    zo = z_other(mid, colour, x0)
+    return [
+        (
+            ref[other, b, x0 - 1 : x1 - 1],
+            ref[other, b, x0 + 1 : x1 + 1],
+            pltpu.roll(mid[b], 1, 1),
+            pltpu.roll(mid[b], REGION_Y - 1, 1),
+            mid[b],
+            zo[b],
         )
-    return out
+        for b in groups
+    ]
 
 
 def split_even(zero, one):
@@ -115,26 +119,54 @@
     return (parts[0] + parts[1]) + parts[2]
 
 
-def kernel(nx, ny, g_ref, c_ref, v_out, r_out, perm, k0, k1, k2, sx0, sy0, rx0, ry0, sx1, sy1, rx1, ry1,
-           ga, gb, vc, cw, sem0, sem1, semx, semy):
+def kernel(nx, ny, g_ref, c_ref, v_out, r_out, perm, k0, d0, v0, g0, k1, d1, v1, g1, k2,
+           sx0, sy0, sc0, rx0, ry0, rc0, sx1, sy1, sc1, rx1, ry1, rc1, ga, gb, vc, cw, sem0, sem1, semx, semy):
     gx, gy = lax.axis_index("gx"), lax.axis_index("gy")
-    has = (gx > 0, gx < nx - 1, gy > 0, gy < ny - 1)
-    peer = ({"gx": gx - 1}, {"gx": gx + 1}, {"gy": gy - 1}, {"gy": gy + 1})
-    bufs = ((sx0, sy0, rx0, ry0, sem0), (sx1, sy1, rx1, ry1, sem1))
-
-    for rx, ry in ((rx0, ry0), (rx1, ry1)):
-        for d in range(4):
-            ref = (rx, ry)[d // 2]
-
-            @pl.when(jnp.logical_not(has[d]))
+    send = ((sx0, sy0, sc0), (sx1, sy1, sc1))
+    recv = ((rx0, ry0, rc0), (rx1, ry1, rc1))
+    sems = (sem0, sem1)
+    size_x, size_y = g_ref.shape[:2]
+    own_x, own_y, ring = (size_x, size_x // 2), (size_y, size_y // 2), (2, 4)
+    near_x = {-1: gx > 0, 0: None, 1: gx < nx - 1}
+    near_y = {-1: gy > 0, 0: None, 1: gy < ny - 1}
+
+    ways = []
+    for dx, dy in ((-1, 0), (1, 0), (0, -1), (0, 1), (-1, -1), (-1, 1), (1, -1), (1, 1)):
+        kind = 2 if dx and dy else (0 if dx else 1)
+        side = {0: (dx + 1) // 2, 1: (dy + 1) // 2, 2: (dx + 1) + (dy + 1) // 2}[kind]
+        if dx and dy:
+            has = jnp.logical_and(near_x[dx], near_y[dy])
+        else:
+            has = near_x[dx] if dx else near_y[dy]
+        target = {}
+        if dx:
+            target["gx"] = gx + dx
+        if dy:
+            target["gy"] = gy + dy
+        ways.append((dx, dy, kind, side, has, target))
+    back = (1, 0, 3, 2, 7, 6, 5, 4)
+
+    for level in range(2):
+        for dx, dy, kind, side, has, target in ways:
+            @pl.when(jnp.logical_not(has))
             def _():
-                ref[:, d % 2] = jnp.zeros((ref.shape[0],) + ref.shape[2:], F32)
+                ref = recv[level][kind]
+                ref[:, side] = jnp.zeros((ref.shape[0],) + ref.shape[2:], F32)
+
+    for ref in (d0, v0, g0, d1, v1, g1):
+        ref[...] = jnp.zeros(ref.shape, F32)
+    for c in range(2):
+        k1[c, 0, 7] = jnp.zeros(k1.shape[3:], F32)
 
     barrier = pltpu.get_barrier_semaphore()
     for s in range(1, nx):
         pl.semaphore_signal(barrier, inc=1, device_id={"gx": lax.rem(gx + s, nx)}, device_id_type=MESH)
     for s in range(1, ny):
         pl.semaphore_signal(barrier, inc=1, device_id={"gy": lax.rem(gy + s, ny)}, device_id_type=MESH)
+    for dx, dy, kind, side, has, target in ways[4:]:
+        @pl.when(has)
+        def _():
+            pl.semaphore_signal(barrier, inc=1, device_id=target, device_id_type=MESH)
 
     size_z = 4 * LANES
     row, col = iota((size_z, size_z), 0), iota((size_z, size_z), 1)
@@ -160,43 +192,64 @@
         first, second = split_even(pair[0], pair[1])
         return [first], [second]
 
-    def copy(level, ph, d, into=False):
-        sx, sy, rx, ry, sem = bufs[level]
-        send, recv = (sx, rx) if d < 2 else (sy, ry)
-        lands = d if into else d + 1 - 2 * (d % 2)
+    def copy(level, ph, d, count, into=False):
+        dx, dy, kind, side, has, target = ways[d]
+        lands = d if into else back[d]
+        sem = sems[level]
         return pltpu.make_async_remote_copy(
-            src_ref=send.at[ph, d % 2], dst_ref=recv.at[ph, lands % 2], send_sem=sem.at[0, ph, d],
-            recv_sem=sem.at[1, ph, lands], device_id=peer[d], device_id_type=MESH)
-
-    def start(level, ph, o):
-        sx, sy = bufs[level][:2]
-        for b, a in enumerate(o):
-            sx[ph, 0, b] = a[:1]
-            sx[ph, 1, b] = a[-1:]
-            sy[ph, 0, b] = a[:, :1]
-            sy[ph, 1, b] = a[:, -1:]
-        for d in range(4):
-            @pl.when(has[d])
+            src_ref=send[level][kind].at[ph, side, pl.ds(0, count)],
+            dst_ref=recv[level][kind].at[ph, ways[lands][3], pl.ds(0, count)],
+            send_sem=sem.at[0, ph, d], recv_sem=sem.at[1, ph, lands], device_id=target, device_id_type=MESH)
+
+    def span(step, own, width, edge):
+        if step == 0:
+            return slice(width, width + own)
+        if edge == "send":
+            return slice(width, 2 * width) if step < 0 else slice(own, own + width)
+        return slice(0, width) if step < 0 else slice(width + own, 2 * width + own)
+
+    def start(level, ph, fields):
+        x, y, h = own_x[level], own_y[level], ring[level]
+        for dx, dy, kind, side, has, target in ways:
+            for f, ref in enumerate(fields):
+                send[level][kind][ph, side, f] = ref[span(dx, x, h, "send"), span(dy, y, h, "send"), :]
+        for d, way in enumerate(ways):
+            @pl.when(way[4])
             def _():
-                copy(level, ph, d).start()
-
-    def finish(level, ph):
-        for d in range(4):
-            @pl.when(has[d])
+                copy(level, ph, d, len(fields)).start()
+
+    def finish(level, ph, fields):
+        x, y, h = own_x[level], own_y[level], ring[level]
+        for d, way in enumerate(ways):
+            @pl.when(way[4])
             def _():
-                copy(level, ph, d, into=True).wait_recv()
-                copy(level, ph, d).wait_send()
-        rx, ry = bufs[level][2:4]
-        groups = range(rx.shape[2])
-        return [[ref[ph, side, b] for b in groups] for ref in (rx, ry) for side in range(2)]
-
-    phase = [0, 0]
-
-    def swap(level, o):
-        ph = phase[level]
-        phase[level] += 1
-        start(level, ph, o)
-        return finish(level, ph)
+                copy(level, ph, d, len(fields), into=True).wait_recv()
+                copy(level, ph, d, len(fields)).wait_send()
+        for dx, dy, kind, side, has, target in ways:
+            for f, ref in enumerate(fields):
+                ref[span(dx, x, h, ""), span(dy, y, h, ""), :] = recv[level][kind][ph, side, f]
+
+    def swap(level, ph, fields):
+        start(level, ph, fields)
+        finish(level, ph, fields)
+
+    def both(ref):
+        return [ref.at[c, b] for c in range(2) for b in range(ref.shape[1])]
+
+    def black(ref):
+        return [ref.at[1, b] for b in range(ref.shape[1])]
+
+    def own(level, a):
+        x, y, h = own_x[level], own_y[level], ring[level]
+        return a[h : h + x, h : h + y]
+
+    def place(level, ref, fields, add=False):
+        x, y, h = own_x[level], own_y[level], ring[level]
+        for c in range(2):
+            for b, a in enumerate(fields[c]):
+                if add:
+                    a = a + ref[c, b, h : h + x, h : h + y]
+                ref[c, b, h : h + x, h : h + y] = a
 
     def gather_copy(stage, s):
         if stage == 0:
@@ -230,70 +283,88 @@
                 device_id={"gy": src}, device_id_type=MESH).wait_recv()
             gather_copy(1, s).wait_send()
 
-    def setup(kref, own, other, halo, colour, scale):
-        for b, near in enumerate(around(other, halo, colour)):
+    def setup(kref, dens, colour, scale):
+        x0, x1 = 1, dens.shape[2] - 1
+        for b, near in enumerate(around(dens, colour, x0, x1)):
+            here = dens[colour, b, x0:x1]
             total = None
             for f in range(6):
-                face = (scale * 0.5) * (own[b] + near[f])
-                kref[colour, b, f] = face
+                face = (scale * 0.5) * (here + near[f])
+                kref[colour, b, f, x0:x1] = face
                 total = face if total is None else total + face
-            kref[colour, b, 6] = total
-            kref[colour, b, 7] = 1.0 / total
-
-    def weigh(kref, o, halo, colour):
+            kref[colour, b, 6, x0:x1] = total
+            kref[colour, b, 7, x0:x1] = jnp.where(here > 0.0, 1.0 / total, 0.0)
+
+    def weigh(kref, v, colour, x0, x1):
         out = []
-        for b, near in enumerate(around(o, halo, colour)):
-            total = kref[colour, b, 0] * near[0]
+        for b, near in enumerate(around(v, colour, x0, x1)):
+            total = kref[colour, b, 0, x0:x1] * near[0]
             for f in range(1, 6):
-                total = total + kref[colour, b, f] * near[f]
+                total = total + kref[colour, b, f, x0:x1] * near[f]
             out.append(total)
         return out
 
-    def update(kref, g, o, halo, colour):
-        n = weigh(kref, o, halo, colour)
-        return [(g[b] + n[b]) * kref[colour, b, 7] for b in range(len(n))]
-
-    def remainder(kref, g, v, o, halo, colour):
-        n = weigh(kref, o, halo, colour)
-        return [g[b] - (kref[colour, b, 6] * v[b] - n[b]) for b in range(len(n))]
-
-    def smooth(level, kref, g, v, sweeps):
-        zero = v is None
-        red, black = (None, None) if zero else v
-        for sweep in range(sweeps):
-            if zero and sweep == 0:
-                red = [g[0][b] * kref[0, b, 7] for b in range(len(g[0]))]
-            else:
-                red = update(kref, g[0], black, swap(level, black), 0)
-            red_halo = swap(level, red)
-            black = update(kref, g[1], red, red_halo, 1)
-        return red, black, red_halo
+    def update(kref, g, v, colour, x0, x1):
+        for b, n in enumerate(weigh(kref, v, colour, x0, x1)):
+            v[colour, b, x0:x1] = (g[colour, b, x0:x1] + n) * kref[colour, b, 7, x0:x1]
+
+    def first(kref, g, v, x0, x1):
+        for b in range(v.shape[1]):
+            v[0, b, x0:x1] = g[0, b, x0:x1] * kref[0, b, 7, x0:x1]
 
     def residual(level, kref, g, v):
-        red, black, red_halo = v
-        left = remainder(kref, g[1], black, red, red_halo, 1)
-        return remainder(kref, g[0], red, black, swap(level, black), 0), left
-
-    pl.semaphore_wait(barrier, nx - 1 + ny - 1)
+        h = ring[level]
+        x0, x1 = h, h + own_x[level]
+        out = []
+        for c in range(2):
+            n = weigh(kref, v, c, x0, x1)
+            out.append([
+                (g[c, b, x0:x1] - (kref[c, b, 6, x0:x1] * v[c, b, x0:x1] - n[b]))[:, h : h + own_y[level]]
+                for b in range(len(n))])
+        return out
+
+    beside_x = (gx > 0).astype(jnp.int32) + (gx < nx - 1).astype(jnp.int32)
+    beside_y = (gy > 0).astype(jnp.int32) + (gy < ny - 1).astype(jnp.int32)
+    pl.semaphore_wait(barrier, nx + ny - 2 + beside_x * beside_y)
 
     dens = unpack(c_ref)
+    place(0, d0, dens)
+    start(0, 0, both(d0))
+    dens_one = coarsen(*dens)
+    place(1, d1, dens_one)
+    start(1, 0, both(d1))
+    dens_two = coarsen(*dens_one)
+    place(0, g0, unpack(g_ref))
+    start(0, 1, both(g0))
+    inverse = [k1.at[c, 0, 7] for c in range(2)]
+    finish(1, 0, both(d1))
     for c in range(2):
-        start(0, c, dens[c])
-    dens_one = coarsen(*dens)
+        setup(k1, d1, c, 0.25)
+    start(1, 1, inverse)
+    finish(0, 0, both(d0))
     for c in range(2):
-        start(1, c, dens_one[c])
-    dens_two = coarsen(*dens_one)
-    source = unpack(g_ref)
-    for level, kref, d, scale in ((0, k0, dens, 1.0), (1, k1, dens_one, 0.25)):
-        halos = [finish(level, c) for c in range(2)]
-        phase[level] = 2
-        for c in range(2):
-            setup(kref, d[c], d[1 - c], halos[1 - c], c, scale)
-
-    fine = smooth(0, k0, source, None, SWEEPS)
-    source_one = coarsen(*residual(0, k0, source, fine))
-    middle = smooth(1, k1, source_one, None, SWEEPS)
-    source_two = coarsen(*residual(1, k1, source_one, middle))
+        setup(k0, d0, c, 1.0)
+    finish(0, 1, both(g0))
+
+    high = 2 + size_x
+    first(k0, g0, v0, 1, high + 1)
+    update(k0, g0, v0, 1, 2, high)
+    for s in range(1, SWEEPS):
+        swap(0, 1 + s, black(v0))
+        update(k0, g0, v0, 0, 1, high + 1)
+        update(k0, g0, v0, 1, 2, high)
+    swap(0, 1 + SWEEPS, black(v0))
+    place(1, g1, coarsen(*residual(0, k0, g0, v0)))
+
+    start(1, 2, both(g1))
+    finish(1, 1, inverse)
+    finish(1, 2, both(g1))
+    wide = v1.shape[2]
+    first(k1, g1, v1, 0, wide)
+    for s in range(1, 2 * SWEEPS):
+        update(k1, g1, v1, s % 2, s, wide - s)
+    start(1, 3, both(v1))
+    source_two = coarsen(*residual(1, k1, g1, v1))
 
     gather(dens_two, source_two)
     for j in range(ny):
@@ -333,15 +404,27 @@
 
     lax.fori_loop(0, COARSE_SWEEPS, sweep, 0)
     field = cw[0]
+    vc[...] = jnp.zeros(vc.shape, F32)
     for j in range(ny):
-        vc[j] = field[:, 2 * j : 2 * j + 2]
-    add = double_rows(vc[gy, pl.ds(2 * gx, 2)])
-    middle = smooth(1, k1, source_one, [[v[0] + add] for v in middle[:2]], SWEEPS)
-    adds = [double_rows(a) for a in split_even(middle[0][0], middle[1][0])]
-    fine = smooth(0, k0, source, [[v[b] + adds[b] for b in range(2)] for v in fine[:2]], SWEEPS)
-    pack(v_out, fine[0], fine[1])
-    left = residual(0, k0, source, fine)
-    pack(r_out, left[0], left[1])
+        vc[1 + j, 2 : 2 + 2 * nx] = field[:, 2 * j : 2 * j + 2]
+    finish(1, 3, both(v1))
+    for dy in range(3):
+        add = double_rows(vc[gy + dy, pl.ds(2 * gx, 6)])
+        for c in range(2):
+            v1[c, 0, :, 4 * dy : 4 * dy + 4] = v1[c, 0, :, 4 * dy : 4 * dy + 4] + add
+    for s in range(2 * SWEEPS):
+        update(k1, g1, v1, s % 2, s + 1, wide - s - 1)
+
+    adds = [double_rows(a) for a in split_even(own(1, v1[0, 0]), own(1, v1[1, 0]))]
+    place(0, v0, [adds, adds], add=True)
+    for s in range(SWEEPS):
+        swap(0, 2 + SWEEPS + s, black(v0))
+        update(k0, g0, v0, 0, 1, high + 1)
+        update(k0, g0, v0, 1, 2, high)
+    start(0, 2 + 2 * SWEEPS, black(v0))
+    pack(v_out, *[[own(0, v0[c, b]) for b in range(2)] for c in range(2)])
+    finish(0, 2 + 2 * SWEEPS, black(v0))
+    pack(r_out, *residual(0, k0, g0, v0))
 
 
 def solution(mesh):
@@ -349,10 +432,21 @@
 
     def shards(right_side, inverse_density):
         x, y, z = right_side.shape
-        x1, y1 = x // 2, y // 2
-        p0, p1 = 4 * SWEEPS + 3, 4 * SWEEPS + 2
-        halo0 = [pltpu.VMEM((p0, 2, 2, 1, y, LANES), F32), pltpu.VMEM((p0, 2, 2, x, 1, LANES), F32)]
-        halo1 = [pltpu.VMEM((p1, 2, 1, 1, y1, LANES), F32), pltpu.VMEM((p1, 2, 1, x1, 1, LANES), F32)]
+        p0, p1 = 3 + 2 * SWEEPS, 4
+
+        def halo(phases, fields, own_x, own_y, ring):
+            return [
+                pltpu.VMEM((phases, 2, fields, ring, own_y, LANES), F32),
+                pltpu.VMEM((phases, 2, fields, own_x, ring, LANES), F32),
+                pltpu.VMEM((phases, 4, fields, ring, ring, LANES), F32),
+            ]
+
+        def level(groups, rows):
+            field = pltpu.VMEM((2, groups, rows, REGION_Y, LANES), F32)
+            return [pltpu.VMEM((2, groups, 8, rows, REGION_Y, LANES), F32), field, field, field]
+
+        halo0 = halo(p0, 4, x, y, 2)
+        halo1 = halo(p1, 2, x // 2, y // 2, 4)
         out = jax.ShapeDtypeStruct(right_side.shape, F32)
         return pl.pallas_call(
             functools.partial(kernel, nx, ny),
@@ -361,16 +455,16 @@
             out_specs=(pl.BlockSpec(memory_space=pltpu.VMEM),) * 2,
             scratch_shapes=[
                 pltpu.VMEM((z, z), jnp.bfloat16),
-                pltpu.VMEM((2, 2, 8, x, y, LANES), F32),
-                pltpu.VMEM((2, 1, 8, x1, y1, LANES), F32),
+                *level(2, x + 4),
+                *level(1, x // 2 + 8),
                 pltpu.VMEM((7, nx * x // 4, ny * y // 4, LANES), F32),
                 *halo0, *halo0, *halo1, *halo1,
                 pltpu.VMEM((nx, 2, x // 4, y // 4, LANES), F32),
                 pltpu.VMEM((ny, 2, nx * x // 4, y // 4, LANES), F32),
-                pltpu.VMEM((ny, nx * x // 4, y // 4, LANES), F32),
+                pltpu.VMEM((ny + 2, nx * x // 4 + 4, y // 4, LANES), F32),
                 pltpu.VMEM((2, nx * x // 4, ny * y // 4, LANES), F32),
-                pltpu.SemaphoreType.DMA((2, p0, 4)),
-                pltpu.SemaphoreType.DMA((2, p1, 4)),
+                pltpu.SemaphoreType.DMA((2, p0, 8)),
+                pltpu.SemaphoreType.DMA((2, p1, 8)),
                 pltpu.SemaphoreType.DMA((2, nx)),
                 pltpu.SemaphoreType.DMA((2, ny)),
             ],

time: 79 us -> 51.9 us (0.66)
  Pallas kernels: 75.1 us -> 48 us
    pallas_call x1, Pallas kernels: 75.1 us -> 48 us  [shards(): pl.pallas_call(functools.partial(kernel, nx, ny), out_shape=(out, out), i...]
where the time goes in v2:
time: 51.9 us; the launch traced here: 51.7 us
  Pallas kernels  48 us (92%)
  local copies, waits for them, and re-layouts  3.11 us (6%)
  between operations  0.65 us (1%)
    pallas_call x1, Pallas kernels, shards(): pl.pallas_call(functools.partial(kernel, nx, ny), out_shape=(out, out), i...  48 us
    unnamed x6, local copies, waits for them, and re-layouts  3.11 us

profile of v2, /device:TPU:0, one launch (start us, length us, event | category | flops | bytes accessed | tf_op | source)
XLA Modules:
  0.0 51.7 jit_solution(5339591742308899916)
XLA Ops:
  0.6 0.0 copy-start
  0.6 0.9 %copy-done = f32[8,8,512]{2,1,0:T(8,128)S(1)} copy-done((f32[8,8,512]{2,1,0:T(8,128)S(1)}, f32[8,8,512]{2,1,0:T(8,128)}, u32[]{:S(2)}) %copy-start) | copy-done | bytes 131096
  1.5 0.0 copy-start.1
  1.5 0.9 %copy-done.1 = f32[8,8,512]{2,1,0:T(8,128)S(1)} copy-done((f32[8,8,512]{2,1,0:T(8,128)S(1)}, f32[8,8,512]{2,1,0:T(8,128)}, u32[]{:S(2)}) %copy-start.1) | copy-done | bytes 131096
  2.4 48.0 %shard_map.41 = (f32[8,8,512]{2,1,0:T(8,128)S(1)}, f32[8,8,512]{2,1,0:T(8,128)S(1)}) custom-call(f32[8,8,512]{2,1,0:T(8,128)S(1)} %copy-done, f32[8,8,512]{2,1,0:T(8,128)S(1)} %copy-done.1), custom_call_target="tpu_custom_call" | custom-call | tf_op jit(solution)/shard_map/pallas_call | solution.py:451
  50.4 0.7 %copy.6 = f32[8,8,512]{2,1,0:T(8,128)} copy(f32[8,8,512]{2,1,0:T(8,128)S(1)} %get-tuple-element.4) | data formatting | bytes 262144
  51.1 0.7 %copy.7 = f32[8,8,512]{2,1,0:T(8,128)} copy(f32[8,8,512]{2,1,0:T(8,128)S(1)} %get-tuple-element.5) | data formatting | bytes 262144
Async XLA Ops:
  0.6 0.9 %copy-start = (f32[8,8,512]{2,1,0:T(8,128)S(1)}, f32[8,8,512]{2,1,0:T(8,128)}, u32[]{:S(2)}) copy-start(f32[8,8,512]{2,1,0:T(8,128)} %g_ref.1) | copy-start | bytes 393220
  1.5 0.9 %copy-start.1 = (f32[8,8,512]{2,1,0:T(8,128)S(1)}, f32[8,8,512]{2,1,0:T(8,128)}, u32[]{:S(2)}) copy-start(f32[8,8,512]{2,1,0:T(8,128)} %c_ref.1) | copy-start | bytes 393220

commit v3 on v2

--- a/solution.py
+++ b/solution.py
@@ -120,7 +120,7 @@
 
 
 def kernel(nx, ny, g_ref, c_ref, v_out, r_out, perm, k0, d0, v0, g0, k1, d1, v1, g1, k2,
-           sx0, sy0, sc0, rx0, ry0, rc0, sx1, sy1, sc1, rx1, ry1, rc1, ga, gb, vc, cw, sem0, sem1, semx, semy):
+           sx0, sy0, sc0, rx0, ry0, rc0, sx1, sy1, sc1, rx1, ry1, rc1, ga, gb, vc, cw, held, sem0, sem1, semx, semy, held_sem):
     gx, gy = lax.axis_index("gx"), lax.axis_index("gy")
     send = ((sx0, sy0, sc0), (sx1, sy1, sc1))
     recv = ((rx0, ry0, rc0), (rx1, ry1, rc1))
@@ -146,17 +146,11 @@
         ways.append((dx, dy, kind, side, has, target))
     back = (1, 0, 3, 2, 7, 6, 5, 4)
 
-    for level in range(2):
-        for dx, dy, kind, side, has, target in ways:
-            @pl.when(jnp.logical_not(has))
-            def _():
-                ref = recv[level][kind]
-                ref[:, side] = jnp.zeros((ref.shape[0],) + ref.shape[2:], F32)
-
-    for ref in (d0, v0, g0, d1, v1, g1):
-        ref[...] = jnp.zeros(ref.shape, F32)
-    for c in range(2):
-        k1[c, 0, 7] = jnp.zeros(k1.shape[3:], F32)
+    loads = [
+        pltpu.make_async_copy(ref, held.at[n], held_sem.at[n]) for n, ref in enumerate((c_ref, g_ref))
+    ]
+    for load in loads:
+        load.start()
 
     barrier = pltpu.get_barrier_semaphore()
     for s in range(1, nx):
@@ -168,6 +162,18 @@
         def _():
             pl.semaphore_signal(barrier, inc=1, device_id=target, device_id_type=MESH)
 
+    for level in range(2):
+        for dx, dy, kind, side, has, target in ways:
+            @pl.when(jnp.logical_not(has))
+            def _():
+                ref = recv[level][kind]
+                ref[:, side] = jnp.zeros((ref.shape[0],) + ref.shape[2:], F32)
+
+    for ref in (d0, v0, g0, d1, v1, g1):
+        ref[...] = jnp.zeros(ref.shape, F32)
+    for c in range(2):
+        k1[c, 0, 7] = jnp.zeros(k1.shape[3:], F32)
+
     size_z = 4 * LANES
     row, col = iota((size_z, size_z), 0), iota((size_z, size_z), 1)
     perm[...] = (row == 4 * (col % LANES) + col // LANES).astype(F32).astype(jnp.bfloat16)
@@ -208,30 +214,30 @@
             return slice(width, 2 * width) if step < 0 else slice(own, own + width)
         return slice(0, width) if step < 0 else slice(width + own, 2 * width + own)
 
-    def start(level, ph, fields):
+    def start(level, ph, fields, count=8):
         x, y, h = own_x[level], own_y[level], ring[level]
-        for dx, dy, kind, side, has, target in ways:
+        for dx, dy, kind, side, has, target in ways[:count]:
             for f, ref in enumerate(fields):
                 send[level][kind][ph, side, f] = ref[span(dx, x, h, "send"), span(dy, y, h, "send"), :]
-        for d, way in enumerate(ways):
+        for d, way in enumerate(ways[:count]):
             @pl.when(way[4])
             def _():
                 copy(level, ph, d, len(fields)).start()
 
-    def finish(level, ph, fields):
+    def finish(level, ph, fields, count=8):
         x, y, h = own_x[level], own_y[level], ring[level]
-        for d, way in enumerate(ways):
+        for d, way in enumerate(ways[:count]):
             @pl.when(way[4])
             def _():
                 copy(level, ph, d, len(fields), into=True).wait_recv()
                 copy(level, ph, d, len(fields)).wait_send()
-        for dx, dy, kind, side, has, target in ways:
+        for dx, dy, kind, side, has, target in ways[:count]:
             for f, ref in enumerate(fields):
                 ref[span(dx, x, h, ""), span(dy, y, h, ""), :] = recv[level][kind][ph, side, f]
 
-    def swap(level, ph, fields):
-        start(level, ph, fields)
-        finish(level, ph, fields)
+    def swap(level, ph, fields, count=8):
+        start(level, ph, fields, count)
+        finish(level, ph, fields, count)
 
     def both(ref):
         return [ref.at[c, b] for c in range(2) for b in range(ref.shape[1])]
@@ -323,19 +329,23 @@
                 for b in range(len(n))])
         return out
 
+    red_source = [g0.at[0, b] for b in range(2)]
+    loads[0].wait()
+    dens = unpack(held.at[0])
+    place(0, d0, dens)
+    dens_one = coarsen(*dens)
+    place(1, d1, dens_one)
+    loads[1].wait()
+    place(0, g0, unpack(held.at[1]))
+
     beside_x = (gx > 0).astype(jnp.int32) + (gx < nx - 1).astype(jnp.int32)
     beside_y = (gy > 0).astype(jnp.int32) + (gy < ny - 1).astype(jnp.int32)
     pl.semaphore_wait(barrier, nx + ny - 2 + beside_x * beside_y)
 
-    dens = unpack(c_ref)
-    place(0, d0, dens)
+    start(1, 0, both(d1))
     start(0, 0, both(d0))
-    dens_one = coarsen(*dens)
-    place(1, d1, dens_one)
-    start(1, 0, both(d1))
+    start(0, 1, red_source)
     dens_two = coarsen(*dens_one)
-    place(0, g0, unpack(g_ref))
-    start(0, 1, both(g0))
     inverse = [k1.at[c, 0, 7] for c in range(2)]
     finish(1, 0, both(d1))
     for c in range(2):
@@ -344,7 +354,7 @@
     finish(0, 0, both(d0))
     for c in range(2):
         setup(k0, d0, c, 1.0)
-    finish(0, 1, both(g0))
+    finish(0, 1, red_source)
 
     high = 2 + size_x
     first(k0, g0, v0, 1, high + 1)
@@ -353,7 +363,7 @@
         swap(0, 1 + s, black(v0))
         update(k0, g0, v0, 0, 1, high + 1)
         update(k0, g0, v0, 1, 2, high)
-    swap(0, 1 + SWEEPS, black(v0))
+    swap(0, 1 + SWEEPS, black(v0), 4)
     place(1, g1, coarsen(*residual(0, k0, g0, v0)))
 
     start(1, 2, both(g1))
@@ -421,9 +431,9 @@
         swap(0, 2 + SWEEPS + s, black(v0))
         update(k0, g0, v0, 0, 1, high + 1)
         update(k0, g0, v0, 1, 2, high)
-    start(0, 2 + 2 * SWEEPS, black(v0))
+    start(0, 2 + 2 * SWEEPS, black(v0), 4)
     pack(v_out, *[[own(0, v0[c, b]) for b in range(2)] for c in range(2)])
-    finish(0, 2 + 2 * SWEEPS, black(v0))
+    finish(0, 2 + 2 * SWEEPS, black(v0), 4)
     pack(r_out, *residual(0, k0, g0, v0))
 
 
@@ -451,7 +461,7 @@
         return pl.pallas_call(
             functools.partial(kernel, nx, ny),
             out_shape=(out, out),
-            in_specs=[pl.BlockSpec(memory_space=pltpu.VMEM)] * 2,
+            in_specs=[pl.BlockSpec(memory_space=pl.ANY)] * 2,
             out_specs=(pl.BlockSpec(memory_space=pltpu.VMEM),) * 2,
             scratch_shapes=[
                 pltpu.VMEM((z, z), jnp.bfloat16),
@@ -463,13 +473,15 @@
                 pltpu.VMEM((ny, 2, nx * x // 4, y // 4, LANES), F32),
                 pltpu.VMEM((ny + 2, nx * x // 4 + 4, y // 4, LANES), F32),
                 pltpu.VMEM((2, nx * x // 4, ny * y // 4, LANES), F32),
+                pltpu.VMEM((2, x, y, z), F32),
                 pltpu.SemaphoreType.DMA((2, p0, 8)),
                 pltpu.SemaphoreType.DMA((2, p1, 8)),
                 pltpu.SemaphoreType.DMA((2, nx)),
                 pltpu.SemaphoreType.DMA((2, ny)),
+                pltpu.SemaphoreType.DMA((2,)),
             ],
             compiler_params=pltpu.CompilerParams(
-                collective_id=0, has_side_effects=True, vmem_limit_bytes=48 * 1024 * 1024
+                collective_id=0, has_side_effects=True, vmem_limit_bytes=60 * 1024 * 1024
             ),
         )(right_side, inverse_density)
 

time: 51.9 us -> 49.5 us (0.954)
  Pallas kernels: 48 us -> 46.4 us
  local copies, waits for them, and re-layouts: 3.11 us -> 2.26 us
    pallas_call x1, Pallas kernels: 48 us -> 46.4 us  [shards(): pl.pallas_call(functools.partial(kernel, nx, ny), out_shape=(out, out), i...]
    unnamed x6 -> x4, local copies, waits for them, and re-layouts: 3.11 us -> 2.26 us
where the time goes in v3:
time: 49.5 us; the launch traced here: 49.3 us
  Pallas kernels  46.4 us (94%)
  local copies, waits for them, and re-layouts  2.26 us (5%)
  between operations  0.65 us (1%)
    pallas_call x1, Pallas kernels, shards(): pl.pallas_call(functools.partial(kernel, nx, ny), out_shape=(out, out), i...  46.4 us
    unnamed x4, local copies, waits for them, and re-layouts  2.26 us

profile of v3, /device:TPU:0, one launch (start us, length us, event | category | flops | bytes accessed | tf_op | source)
XLA Modules:
  0.0 49.3 jit_solution(6028591284909179211)
XLA Ops:
  0.6 46.4 %shard_map.41 = (f32[8,8,512]{2,1,0:T(8,128)}, f32[8,8,512]{2,1,0:T(8,128)}) custom-call(f32[8,8,512]{2,1,0:T(8,128)} %g_ref.1, f32[8,8,512]{2,1,0:T(8,128)} %c_ref.1), custom_call_target="tpu_custom_call" | custom-call | tf_op jit(solution)/shard_map/pallas_call | solution.py:461
  47.0 0.0 copy-start
  47.0 1.6 %copy.6 = f32[8,8,512]{2,1,0:T(8,128)} copy(f32[8,8,512]{2,1,0:T(8,128)} %get-tuple-element.4) | data formatting | bytes 262144
  48.7 0.0 copy-done
  48.7 0.7 %copy.7 = f32[8,8,512]{2,1,0:T(8,128)} copy(f32[8,8,512]{2,1,0:T(8,128)S(1)} %copy-done) | data formatting | bytes 262144
Async XLA Ops:
  47.0 1.6 %copy-start = (f32[8,8,512]{2,1,0:T(8,128)S(1)}, f32[8,8,512]{2,1,0:T(8,128)}, u32[]{:S(2)}) copy-start(f32[8,8,512]{2,1,0:T(8,128)} %get-tuple-element.5) | copy-start | bytes 393220

commit v4 on v3

--- a/solution.py
+++ b/solution.py
@@ -126,7 +126,7 @@
     recv = ((rx0, ry0, rc0), (rx1, ry1, rc1))
     sems = (sem0, sem1)
     size_x, size_y = g_ref.shape[:2]
-    own_x, own_y, ring = (size_x, size_x // 2), (size_y, size_y // 2), (2, 4)
+    own_x, own_y, ring = (size_x, size_x // 2), (size_y, size_y // 2), (3, 4)
     near_x = {-1: gx > 0, 0: None, 1: gx < nx - 1}
     near_y = {-1: gy > 0, 0: None, 1: gy < ny - 1}
 
@@ -329,7 +329,6 @@
                 for b in range(len(n))])
         return out
 
-    red_source = [g0.at[0, b] for b in range(2)]
     loads[0].wait()
     dens = unpack(held.at[0])
     place(0, d0, dens)
@@ -344,7 +343,7 @@
 
     start(1, 0, both(d1))
     start(0, 0, both(d0))
-    start(0, 1, red_source)
+    start(0, 1, both(g0))
     dens_two = coarsen(*dens_one)
     inverse = [k1.at[c, 0, 7] for c in range(2)]
     finish(1, 0, both(d1))
@@ -354,16 +353,20 @@
     finish(0, 0, both(d0))
     for c in range(2):
         setup(k0, d0, c, 1.0)
-    finish(0, 1, red_source)
-
-    high = 2 + size_x
-    first(k0, g0, v0, 1, high + 1)
-    update(k0, g0, v0, 1, 2, high)
+    finish(0, 1, both(g0))
+
+    low, high = ring[0], ring[0] + size_x
+
+    def fine_sweep(ph, last):
+        more = 1 if last else 0
+        swap(0, ph, black(v0))
+        update(k0, g0, v0, 0, low - 1 - more, high + 1 + more)
+        update(k0, g0, v0, 1, low - more, high + more)
+
+    first(k0, g0, v0, low - 1, high + 1)
+    update(k0, g0, v0, 1, low, high)
     for s in range(1, SWEEPS):
-        swap(0, 1 + s, black(v0))
-        update(k0, g0, v0, 0, 1, high + 1)
-        update(k0, g0, v0, 1, 2, high)
-    swap(0, 1 + SWEEPS, black(v0), 4)
+        fine_sweep(1 + s, s == SWEEPS - 1)
     place(1, g1, coarsen(*residual(0, k0, g0, v0)))
 
     start(1, 2, both(g1))
@@ -428,12 +431,8 @@
     adds = [double_rows(a) for a in split_even(own(1, v1[0, 0]), own(1, v1[1, 0]))]
     place(0, v0, [adds, adds], add=True)
     for s in range(SWEEPS):
-        swap(0, 2 + SWEEPS + s, black(v0))
-        update(k0, g0, v0, 0, 1, high + 1)
-        update(k0, g0, v0, 1, 2, high)
-    start(0, 2 + 2 * SWEEPS, black(v0), 4)
+        fine_sweep(2 + SWEEPS + s, s == SWEEPS - 1)
     pack(v_out, *[[own(0, v0[c, b]) for b in range(2)] for c in range(2)])
-    finish(0, 2 + 2 * SWEEPS, black(v0), 4)
     pack(r_out, *residual(0, k0, g0, v0))
 
 
@@ -455,7 +454,7 @@
             field = pltpu.VMEM((2, groups, rows, REGION_Y, LANES), F32)
             return [pltpu.VMEM((2, groups, 8, rows, REGION_Y, LANES), F32), field, field, field]
 
-        halo0 = halo(p0, 4, x, y, 2)
+        halo0 = halo(p0, 4, x, y, 3)
         halo1 = halo(p1, 2, x // 2, y // 2, 4)
         out = jax.ShapeDtypeStruct(right_side.shape, F32)
         return pl.pallas_call(
@@ -465,7 +464,7 @@
             out_specs=(pl.BlockSpec(memory_space=pltpu.VMEM),) * 2,
             scratch_shapes=[
                 pltpu.VMEM((z, z), jnp.bfloat16),
-                *level(2, x + 4),
+                *level(2, x + 6),
                 *level(1, x // 2 + 8),
                 pltpu.VMEM((7, nx * x // 4, ny * y // 4, LANES), F32),
                 *halo0, *halo0, *halo1, *halo1,

time: 49.5 us -> 47.5 us (0.960)
  Pallas kernels: 46.4 us -> 44.5 us
    pallas_call x1, Pallas kernels: 46.4 us -> 44.5 us  [shards(): pl.pallas_call(functools.partial(kernel, nx, ny), out_shape=(out, out), i...]
where the time goes in v4:
time: 47.5 us; the launch traced here: 47.4 us
  Pallas kernels  44.5 us (94%)
  local copies, waits for them, and re-layouts  2.26 us (5%)
  between operations  0.65 us (1%)
    pallas_call x1, Pallas kernels, shards(): pl.pallas_call(functools.partial(kernel, nx, ny), out_shape=(out, out), i...  44.5 us
    unnamed x4, local copies, waits for them, and re-layouts  2.26 us

profile of v4, /device:TPU:0, one launch (start us, length us, event | category | flops | bytes accessed | tf_op | source)
XLA Modules:
  0.0 47.4 jit_solution(5004364259868826748)
XLA Ops:
  0.6 44.5 %shard_map.41 = (f32[8,8,512]{2,1,0:T(8,128)}, f32[8,8,512]{2,1,0:T(8,128)}) custom-call(f32[8,8,512]{2,1,0:T(8,128)} %g_ref.1, f32[8,8,512]{2,1,0:T(8,128)} %c_ref.1), custom_call_target="tpu_custom_call" | custom-call | tf_op jit(solution)/shard_map/pallas_call | solution.py:460
  45.1 0.0 copy-start
  45.1 1.6 %copy.6 = f32[8,8,512]{2,1,0:T(8,128)} copy(f32[8,8,512]{2,1,0:T(8,128)} %get-tuple-element.4) | data formatting | bytes 262144
  46.7 0.0 copy-done
  46.7 0.7 %copy.7 = f32[8,8,512]{2,1,0:T(8,128)} copy(f32[8,8,512]{2,1,0:T(8,128)S(1)} %copy-done) | data formatting | bytes 262144
Async XLA Ops:
  45.1 1.6 %copy-start = (f32[8,8,512]{2,1,0:T(8,128)S(1)}, f32[8,8,512]{2,1,0:T(8,128)}, u32[]{:S(2)}) copy-start(f32[8,8,512]{2,1,0:T(8,128)} %get-tuple-element.5) | copy-start | bytes 393220

commit v5 on v4

--- a/solution.py
+++ b/solution.py
@@ -120,7 +120,7 @@
 
 
 def kernel(nx, ny, g_ref, c_ref, v_out, r_out, perm, k0, d0, v0, g0, k1, d1, v1, g1, k2,
-           sx0, sy0, sc0, rx0, ry0, rc0, sx1, sy1, sc1, rx1, ry1, rc1, ga, gb, vc, cw, held, sem0, sem1, semx, semy, held_sem):
+           sx0, sy0, sc0, rx0, ry0, rc0, sx1, sy1, sc1, rx1, ry1, rc1, ga, vc, cw, held, sem0, sem1, sem_all, held_sem):
     gx, gy = lax.axis_index("gx"), lax.axis_index("gy")
     send = ((sx0, sy0, sc0), (sx1, sy1, sc1))
     recv = ((rx0, ry0, rc0), (rx1, ry1, rc1))
@@ -153,14 +153,10 @@
         load.start()
 
     barrier = pltpu.get_barrier_semaphore()
-    for s in range(1, nx):
-        pl.semaphore_signal(barrier, inc=1, device_id={"gx": lax.rem(gx + s, nx)}, device_id_type=MESH)
-    for s in range(1, ny):
-        pl.semaphore_signal(barrier, inc=1, device_id={"gy": lax.rem(gy + s, ny)}, device_id_type=MESH)
-    for dx, dy, kind, side, has, target in ways[4:]:
-        @pl.when(has)
-        def _():
-            pl.semaphore_signal(barrier, inc=1, device_id=target, device_id_type=MESH)
+    others = [(a, b) for b in range(ny) for a in range(nx) if a or b]
+    for a, b in others:
+        target = {"gx": lax.rem(gx + a, nx), "gy": lax.rem(gy + b, ny)}
+        pl.semaphore_signal(barrier, inc=1, device_id=target, device_id_type=MESH)
 
     for level in range(2):
         for dx, dy, kind, side, has, target in ways:
@@ -230,10 +226,12 @@
             @pl.when(way[4])
             def _():
                 copy(level, ph, d, len(fields), into=True).wait_recv()
-                copy(level, ph, d, len(fields)).wait_send()
+        sent.append((level, ph, len(fields)))
         for dx, dy, kind, side, has, target in ways[:count]:
             for f, ref in enumerate(fields):
                 ref[span(dx, x, h, ""), span(dy, y, h, ""), :] = recv[level][kind][ph, side, f]
+
+    sent = []
 
     def swap(level, ph, fields, count=8):
         start(level, ph, fields, count)
@@ -257,37 +255,19 @@
                     a = a + ref[c, b, h : h + x, h : h + y]
                 ref[c, b, h : h + x, h : h + y] = a
 
-    def gather_copy(stage, s):
-        if stage == 0:
-            return pltpu.make_async_remote_copy(
-                src_ref=ga.at[gx], dst_ref=ga.at[gx], send_sem=semx.at[0, s], recv_sem=semx.at[1, s],
-                device_id={"gx": lax.rem(gx + s, nx)}, device_id_type=MESH)
+    def gather_copy(a, b, into=False):
+        slot = ga.at[lax.rem(gy + ny - b, ny), lax.rem(gx + nx - a, nx)] if into else ga.at[gy, gx]
         return pltpu.make_async_remote_copy(
-            src_ref=gb.at[gy], dst_ref=gb.at[gy], send_sem=semy.at[0, s], recv_sem=semy.at[1, s],
-            device_id={"gy": lax.rem(gy + s, ny)}, device_id_type=MESH)
+            src_ref=slot, dst_ref=slot, send_sem=sem_all.at[0, b, a], recv_sem=sem_all.at[1, b, a],
+            device_id={"gx": lax.rem(gx + a, nx), "gy": lax.rem(gy + b, ny)}, device_id_type=MESH)
 
     def gather(dens, source):
-        ga[gx, 0] = dens
-        ga[gx, 1] = source
-        for s in range(1, nx):
-            gather_copy(0, s).start()
-        for s in range(1, nx):
-            src = lax.rem(gx + nx - s, nx)
-            pltpu.make_async_remote_copy(
-                src_ref=ga.at[src], dst_ref=ga.at[src], send_sem=semx.at[0, s], recv_sem=semx.at[1, s],
-                device_id={"gx": src}, device_id_type=MESH).wait_recv()
-            gather_copy(0, s).wait_send()
-        for i in range(nx):
-            gb[gy, 0, 2 * i : 2 * i + 2] = ga[i, 0]
-            gb[gy, 1, 2 * i : 2 * i + 2] = ga[i, 1]
-        for s in range(1, ny):
-            gather_copy(1, s).start()
-        for s in range(1, ny):
-            src = lax.rem(gy + ny - s, ny)
-            pltpu.make_async_remote_copy(
-                src_ref=gb.at[src], dst_ref=gb.at[src], send_sem=semy.at[0, s], recv_sem=semy.at[1, s],
-                device_id={"gy": src}, device_id_type=MESH).wait_recv()
-            gather_copy(1, s).wait_send()
+        ga[gy, gx, 0] = dens
+        ga[gy, gx, 1] = source
+        for a, b in reversed(others):
+            gather_copy(a, b).start()
+        for a, b in reversed(others):
+            gather_copy(a, b, into=True).wait_recv()
 
     def setup(kref, dens, colour, scale):
         x0, x1 = 1, dens.shape[2] - 1
@@ -337,9 +317,7 @@
     loads[1].wait()
     place(0, g0, unpack(held.at[1]))
 
-    beside_x = (gx > 0).astype(jnp.int32) + (gx < nx - 1).astype(jnp.int32)
-    beside_y = (gy > 0).astype(jnp.int32) + (gy < ny - 1).astype(jnp.int32)
-    pl.semaphore_wait(barrier, nx + ny - 2 + beside_x * beside_y)
+    pl.semaphore_wait(barrier, nx * ny - 1)
 
     start(1, 0, both(d1))
     start(0, 0, both(d0))
@@ -381,8 +359,9 @@
 
     gather(dens_two, source_two)
     for j in range(ny):
-        cw[0, :, 2 * j : 2 * j + 2] = gb[j, 0]
-        cw[1, :, 2 * j : 2 * j + 2] = gb[j, 1]
+        for i in range(nx):
+            for n in range(2):
+                cw[n, 2 * i : 2 * i + 2, 2 * j : 2 * j + 2] = ga[j, i, n]
 
     def sides(a):
         plane = jnp.zeros_like(a[:1])
@@ -434,6 +413,13 @@
         fine_sweep(2 + SWEEPS + s, s == SWEEPS - 1)
     pack(v_out, *[[own(0, v0[c, b]) for b in range(2)] for c in range(2)])
     pack(r_out, *residual(0, k0, g0, v0))
+    for d, way in enumerate(ways):
+        @pl.when(way[4])
+        def _():
+            for level, ph, fields in sent:
+                copy(level, ph, d, fields).wait_send()
+    for a, b in others:
+        gather_copy(a, b).wait_send()
 
 
 def solution(mesh):
@@ -468,15 +454,13 @@
                 *level(1, x // 2 + 8),
                 pltpu.VMEM((7, nx * x // 4, ny * y // 4, LANES), F32),
                 *halo0, *halo0, *halo1, *halo1,
-                pltpu.VMEM((nx, 2, x // 4, y // 4, LANES), F32),
-                pltpu.VMEM((ny, 2, nx * x // 4, y // 4, LANES), F32),
+                pltpu.VMEM((ny, nx, 2, x // 4, y // 4, LANES), F32),
                 pltpu.VMEM((ny + 2, nx * x // 4 + 4, y // 4, LANES), F32),
                 pltpu.VMEM((2, nx * x // 4, ny * y // 4, LANES), F32),
                 pltpu.VMEM((2, x, y, z), F32),
                 pltpu.SemaphoreType.DMA((2, p0, 8)),
                 pltpu.SemaphoreType.DMA((2, p1, 8)),
-                pltpu.SemaphoreType.DMA((2, nx)),
-                pltpu.SemaphoreType.DMA((2, ny)),
+                pltpu.SemaphoreType.DMA((2, ny, nx)),
                 pltpu.SemaphoreType.DMA((2,)),
             ],
             compiler_params=pltpu.CompilerParams(

time: 47.5 us -> 48.4 us (1.019)
  Pallas kernels: 44.5 us -> 45.4 us
    pallas_call x1, Pallas kernels: 44.5 us -> 45.4 us  [shards(): pl.pallas_call(functools.partial(kernel, nx, ny), out_shape=(out, out), i...]
where the time goes in v5:
time: 48.4 us; the launch traced here: 48.3 us
  Pallas kernels  45.4 us (94%)
  local copies, waits for them, and re-layouts  2.26 us (5%)
  between operations  0.65 us (1%)
    pallas_call x1, Pallas kernels, shards(): pl.pallas_call(functools.partial(kernel, nx, ny), out_shape=(out, out), i...  45.4 us
    unnamed x4, local copies, waits for them, and re-layouts  2.26 us

profile of v5, /device:TPU:0, one launch (start us, length us, event | category | flops | bytes accessed | tf_op | source)
XLA Modules:
  0.0 48.3 jit_solution(7876431445029139829)
XLA Ops:
  0.6 45.4 %shard_map.41 = (f32[8,8,512]{2,1,0:T(8,128)}, f32[8,8,512]{2,1,0:T(8,128)}) custom-call(f32[8,8,512]{2,1,0:T(8,128)} %g_ref.1, f32[8,8,512]{2,1,0:T(8,128)} %c_ref.1), custom_call_target="tpu_custom_call" | custom-call | tf_op jit(solution)/shard_map/pallas_call | solution.py:446
  46.0 0.0 copy-start
  46.0 1.6 %copy.6 = f32[8,8,512]{2,1,0:T(8,128)} copy(f32[8,8,512]{2,1,0:T(8,128)} %get-tuple-element.4) | data formatting | bytes 262144
  47.6 0.0 copy-done
  47.6 0.7 %copy.7 = f32[8,8,512]{2,1,0:T(8,128)} copy(f32[8,8,512]{2,1,0:T(8,128)S(1)} %copy-done) | data formatting | bytes 262144
Async XLA Ops:
  46.0 1.6 %copy-start = (f32[8,8,512]{2,1,0:T(8,128)S(1)}, f32[8,8,512]{2,1,0:T(8,128)}, u32[]{:S(2)}) copy-start(f32[8,8,512]{2,1,0:T(8,128)} %get-tuple-element.5) | copy-start | bytes 393220
